TPU v7x, 32 devices: a whole 2x2x4 slice. The times are simulated.
32 devices in a mesh: row: 8 (over z, y), col: 4 (over x, core).
Axes of the slice: x: 2, y: 2, z: 4, core: 2. Of those that a mesh axis runs over, the one named last changes fastest.
Arguments:
- node_latent: bfloat16 [8192, 512], P(('row', 'col')), may hold values from -6 to 6
- edge_latent: bfloat16 [65536, 512], P(('row', 'col')), may hold values from -6 to 6
- node_cotangent: bfloat16 [8192, 512], P(('row', 'col')), may hold values from -6 to 6
- edge_cotangent: bfloat16 [65536, 512], P(('row', 'col')), may hold values from -6 to 6
- w_edge_in: bfloat16 [1536, 512], replicated, may hold values from -0.15625 to 0.15625
- w_edge_out: bfloat16 [512, 512], replicated, may hold values from -0.25 to 0.25
- w_node_in: bfloat16 [1024, 512], replicated, may hold values from -0.1875 to 0.1875
- w_node_out: bfloat16 [512, 512], replicated, may hold values from -0.25 to 0.25
- sender_code: int32 [65536], P(('row', 'col')), may hold values from 0 to 767, as said below
- receiver: int32 [65536], P(('row', 'col')), may hold values from 0 to 255
- near_list: int32 [32, 4, 64], P(('row', 'col')), may hold values from 0 to 255
- far_list: int32 [32, 32, 8], P(('row', 'col')), may hold values from 0 to 255
Outputs:
- node_new: bfloat16 [8192, 512], P(('row', 'col'))
- edge_new: bfloat16 [65536, 512], P(('row', 'col'))
- grad_node: bfloat16 [8192, 512], P(('row', 'col'))
- grad_edge: bfloat16 [65536, 512], P(('row', 'col'))
- grad_edge_in: float32 [1536, 512], P(('row', 'col'))
- grad_edge_out: float32 [512, 512], P(('row', 'col'))
- grad_node_in: float32 [1024, 512], P(('row', 'col'))
- grad_node_out: float32 [512, 512], P(('row', 'col'))
Inputs may be any that keep to these rules, and one draw needn't show every extreme that they name: `sender_code`: for each block d and each device p, the far codes of block d that name p use the first c of the 8 slots, 1 <= c <= 8, c drawn for each pair, and every block uses all 8 slots of some device. Every local code, every near code and every used far code is read by at least one edge of its block.
All inputs are finite; a program needn't handle non-finite values.
Results may differ from a plain program's by a relative error of at most 0.015.
Values may be sent and summed in bfloat16 or wider, within the bound.
A program may use at most 128 MiB of HBM per device.

v0:
```python
import math

import jax
import jax.numpy as jnp
from jax import lax
from jax.sharding import PartitionSpec as P

EPS = 1e-05


def passed_along(value, axis, by):
    peers = lax.axis_size(axis)
    return lax.ppermute(value, axis, [(i, (i + by) % peers) for i in range(peers)])


def shortened(value):
    return jax.tree.map(lambda a: a.astype(jnp.bfloat16) if a.dtype == jnp.float32 else a, value)


def layer_norm(value):
    mean = jnp.mean(value, -1, keepdims=True)
    centred = value - mean
    recip = lax.rsqrt(jnp.mean(centred * centred, -1, keepdims=True) + EPS)
    return centred * recip


def norm_grad(value, grad):
    mean = jnp.mean(value, -1, keepdims=True)
    centred = value - mean
    recip = lax.rsqrt(jnp.mean(centred * centred, -1, keepdims=True) + EPS)
    normed = centred * recip
    inner = (
        grad
        - jnp.mean(grad, -1, keepdims=True)
        - normed * jnp.mean(grad * normed, -1, keepdims=True)
    )
    return recip * inner


def silu_grad(value):
    sigma = jax.nn.sigmoid(value)
    return sigma * (1.0 + value * (1.0 - sigma))


def plain_dot(left, right):
    return jnp.dot(left, right, preferred_element_type=jnp.float32)


def exact_dot(left, right):
    return jnp.dot(left, right, precision=lax.Precision.HIGHEST, preferred_element_type=jnp.float32)


def back_dot(left, weight):
    return lax.dot_general(
        left, weight, (((1,), (1,)), ((), ())), preferred_element_type=jnp.float32
    )


def exact_back(left, weight):
    return lax.dot_general(
        left,
        weight.astype(jnp.float32),
        (((1,), (1,)), ((), ())),
        precision=lax.Precision.HIGHEST,
        preferred_element_type=jnp.float32,
    )


def cross_dot(left, right):
    return lax.dot_general(
        left, right, (((0,), (0,)), ((), ())), preferred_element_type=jnp.float32
    )


def shards(
    node_latent,
    edge_latent,
    node_cotangent,
    edge_cotangent,
    w_edge_in,
    w_edge_out,
    w_node_in,
    w_node_out,
    sender_code,
    receiver,
    near_list,
    far_list,
):
    node_rows, width = node_latent.shape
    edge_rows = edge_latent.shape[0]
    rows_grid = lax.axis_size("row")
    cols_grid = lax.axis_size("col")
    peers = rows_grid * cols_grid
    near_lists = near_list[0]
    far_lists = far_list[0]
    near_width = near_lists.shape[1]
    far_width = far_lists.shape[1]
    steps_row = ((0, 1), (1, -1))
    steps_col = ((2, 1), (3, -1))
    near_send = jnp.take(node_latent, near_lists, axis=0)
    near_parts = []
    for slot_index, offset in steps_row:
        near_parts.append(passed_along(near_send[slot_index], "row", offset))
    for slot_index, offset in steps_col:
        near_parts.append(passed_along(near_send[slot_index], "col", offset))
    far_send = jnp.take(node_latent, far_lists, axis=0)
    far_recv = lax.all_to_all(far_send, ("row", "col"), split_axis=0, concat_axis=0, tiled=True)
    far_recv = far_recv.reshape(peers * far_width, width)
    table = jnp.concatenate([node_latent] + near_parts + [far_recv], 0)
    table_rows = table.shape[0]
    w_e = w_edge_in[:width]
    w_s = w_edge_in[width : 2 * width]
    w_r = w_edge_in[2 * width :]
    sent_rows = jnp.take(table, sender_code, axis=0)
    recv_rows = jnp.take(node_latent, receiver, axis=0)
    edge_pre = plain_dot(edge_latent, w_e) + plain_dot(sent_rows, w_s) + plain_dot(recv_rows, w_r)
    edge_hidden = jax.nn.silu(edge_pre).astype(jnp.bfloat16)
    edge_mid = plain_dot(edge_hidden, w_edge_out)
    edge_new = (edge_latent.astype(jnp.float32) + layer_norm(edge_mid)).astype(jnp.bfloat16)
    node_ids = jnp.arange(node_rows, dtype=jnp.int32)[:, None]
    onehot = (receiver[None, :] == node_ids).astype(jnp.bfloat16)
    gathered = plain_dot(onehot, edge_new).astype(jnp.bfloat16)
    node_pre = plain_dot(node_latent, w_node_in[:width]) + plain_dot(gathered, w_node_in[width:])
    node_hidden = jax.nn.silu(node_pre).astype(jnp.bfloat16)
    node_mid = plain_dot(node_hidden, w_node_out)
    node_new = (node_latent.astype(jnp.float32) + layer_norm(node_mid)).astype(jnp.bfloat16)
    node_delta = norm_grad(node_mid, node_cotangent.astype(jnp.float32)).astype(jnp.bfloat16)
    node_pre_delta = (back_dot(node_delta, w_node_out) * silu_grad(node_pre)).astype(jnp.bfloat16)
    gathered_grad = back_dot(node_pre_delta, w_node_in[width:])
    node_in_grad = back_dot(node_pre_delta, w_node_in[:width])
    grad_node_in = jnp.concatenate(
        [cross_dot(node_latent, node_pre_delta), cross_dot(gathered, node_pre_delta)], 0
    )
    grad_node_out = cross_dot(node_hidden, node_delta)
    edge_total = edge_cotangent.astype(jnp.float32) + jnp.take(gathered_grad, receiver, axis=0)
    edge_delta = norm_grad(edge_mid, edge_total).astype(jnp.bfloat16)
    edge_pre_delta = (back_dot(edge_delta, w_edge_out) * silu_grad(edge_pre)).astype(jnp.bfloat16)
    grad_edge = (edge_total + back_dot(edge_pre_delta, w_e)).astype(jnp.bfloat16)
    grad_edge_in = jnp.concatenate(
        [
            cross_dot(edge_latent, edge_pre_delta),
            cross_dot(sent_rows, edge_pre_delta),
            cross_dot(recv_rows, edge_pre_delta),
        ],
        0,
    )
    grad_edge_out = cross_dot(edge_hidden, edge_delta)
    code_ids = jnp.arange(table_rows, dtype=jnp.int32)[:, None]
    code_onehot = (sender_code[None, :] == code_ids).astype(jnp.bfloat16)
    code_sums = plain_dot(code_onehot, edge_pre_delta)
    table_grad = exact_back(code_sums, w_s)
    recv_sums = plain_dot(onehot, edge_pre_delta)
    node_total = node_cotangent.astype(jnp.float32) + node_in_grad + table_grad[:node_rows]
    node_total = node_total + exact_back(recv_sums, w_r)
    near_grad = table_grad[node_rows : node_rows + 4 * near_width].reshape(4, near_width, width)
    returned_parts = []
    for slot_index, offset in steps_row:
        returned_parts.append(
            passed_along(near_grad[slot_index].astype(jnp.bfloat16), "row", -offset).astype(
                jnp.float32
            )
        )
    for slot_index, offset in steps_col:
        returned_parts.append(
            passed_along(near_grad[slot_index].astype(jnp.bfloat16), "col", -offset).astype(
                jnp.float32
            )
        )
    far_grad = table_grad[node_rows + 4 * near_width :].reshape(peers, far_width, width)
    far_back = lax.all_to_all(
        far_grad.astype(jnp.bfloat16), ("row", "col"), split_axis=0, concat_axis=0, tiled=True
    ).astype(far_grad.dtype)
    far_back = far_back.reshape(peers * far_width, width)
    returned_rows = jnp.concatenate(returned_parts + [far_back], 0)
    owner_index = jnp.concatenate([near_lists.reshape(-1), far_lists.reshape(-1)], 0)
    owner_onehot = (owner_index[None, :] == node_ids).astype(jnp.float32)
    node_total = node_total + exact_dot(owner_onehot, returned_rows)
    grad_node = node_total.astype(jnp.bfloat16)
    edge_scale = 1.0 / math.sqrt(edge_rows * peers)
    node_scale = 1.0 / math.sqrt(node_rows * peers)
    grads = (
        grad_edge_in * edge_scale,
        grad_edge_out * edge_scale,
        grad_node_in * node_scale,
        grad_node_out * node_scale,
    )
    shaped = tuple(
        (item.reshape(rows_grid, cols_grid, item.shape[0] // peers, width) for item in grads)
    )
    partial_sums = jax.tree.map(
        lambda part: part.astype(jnp.float32),
        lax.psum_scatter(shortened(shaped), "col", scatter_dimension=1, tiled=True),
    )
    summed = jax.tree.map(
        lambda part: part.astype(jnp.float32),
        lax.psum_scatter(shortened(partial_sums), "row", scatter_dimension=0, tiled=True),
    )
    summed = tuple((item.reshape(item.shape[2], width) for item in summed))
    return (node_new, edge_new, grad_node, grad_edge, summed[0], summed[1], summed[2], summed[3])


def solution(mesh):
    in_specs = (
        P(("row", "col"), None),
        P(("row", "col"), None),
        P(("row", "col"), None),
        P(("row", "col"), None),
        P(),
        P(),
        P(),
        P(),
        P(("row", "col")),
        P(("row", "col")),
        P(("row", "col"), None, None),
        P(("row", "col"), None, None),
    )
    out_specs = (
        P(("row", "col"), None),
        P(("row", "col"), None),
        P(("row", "col"), None),
        P(("row", "col"), None),
        P(("row", "col"), None),
        P(("row", "col"), None),
        P(("row", "col"), None),
        P(("row", "col"), None),
    )
    return jax.shard_map(shards, mesh=mesh, in_specs=in_specs, out_specs=out_specs, check_vma=False)
```

profile of v0, /device:TPU:0, one launch (start us, length us, event | category | flops | bytes accessed | tf_op | source)
XLA Modules:
  0.0 481.4 jit_solution(9737728634486707445)
XLA Ops:
  15.7 3.1 collective-permute-start.1
  22.6 3.3 all-to-all-start
  26.6 4.9 %fusion.34 = f32[2048,512]{1,0:T(8,128)} fusion(bf16[2048,512]{1,0:T(8,128)(2,1)} %param.13, bf16[1536,512]{1,0:T(8,128)(2,1)} %param.16), kind=kOutput, calls=%fused_computation.74 | convolution fusion | flops 1073741824 | bytes 6815744 | tf_op jit(solution)/shard_map/dot_general | solution.py:46
  31.5 4.1 copy.40
  35.6 9.2 %gather_fusion.3 = bf16[2048,512]{1,0:T(8,128)(2,1)} fusion(bf16[256,512]{1,0:T(8,128)(2,1)S(1)} %copy-done.1, s32[2048]{0:T(1024)S(1)} %fusion.41), kind=kCustom, calls=%fused_computation.3 | custom fusion | bytes 4202496 | tf_op jit(solution)/shard_map/jit(_take)/gather | solution.py:115
  44.8 4.0 copy.44
  48.7 4.0 copy.45
  55.9 9.2 %gather_fusion.2 = bf16[2048,512]{1,0:T(8,128)(2,1)} fusion(bf16[768,512]{1,0:T(8,128)(2,1)S(1)} %bitcast_dynamic-update-slice_fusion.1, s32[2048]{0:T(1024)S(1)} %fusion.40), kind=kCustom, calls=%fused_computation.2 | custom fusion | bytes 4202496 | tf_op jit(solution)/shard_map/jit(_take)/gather | solution.py:114
  65.1 4.1 copy.43
  69.2 3.0 fusion.7
  72.7 4.2 multiply_convert_fusion.2
  92.3 8.9 %gather_fusion.4 = f32[2048,512]{1,0:T(8,128)} fusion(f32[256,512]{1,0:T(8,128)S(1)} %fusion.25, s32[2048]{0:T(1024)S(1)} %fusion.41), kind=kCustom, calls=%fused_computation.4 | custom fusion | bytes 8396800 | tf_op jit(solution)/shard_map/jit(_take)/gather | solution.py:135
  101.2 5.5 %copy.46 = f32[2048,512]{0,1:T(8,128)} copy(f32[2048,512]{1,0:T(8,128)} %gather_fusion.4) | data formatting | bytes 8388608 | tf_op jit(solution)/shard_map/jit(_take)/gather | solution.py:135
  106.7 4.9 %fusion.47 = (f32[2048]{0:T(1024)S(1)}, f32[2048]{0:T(1024)S(1)}) fusion(f32[2048,512]{0,1:T(8,128)} %copy.46, pred[2048]{0:T(1024)(128)(4,1)S(1)} %compare_and_fusion, bf16[2048,512]{0,1:T(8,128)(2,1)S(1)} %copy-done.5, f32[2048]{0:T(1024)S(1)} %add_rsqrt_fusion, f32[2048,512]{0,1:T(8,128)} %copy-done.2, f32[2048]{0:T(1024)S(1)} %broadcast_multiply_fusion.2), kind=kLoop, calls=%fused_computation.134 | loop fusion | flops 8384512 | bytes 10520576 | tf_op jit(solution)/shard_map/reduce_sum | solution.py:34
  132.5 4.2 fusion.51
  137.3 4.6 collective-permute-start.4
  143.5 6.1 %all-to-all-start.1 = ((bf16[32,8,512]{2,1,0:T(8,128)(2,1)}), bf16[32,8,512]{2,1,0:T(8,128)(2,1)}, u32[]{:S(2)}, u32[]{:S(2)}) async-start(bf16[32,8,512]{2,1,0:T(8,128)(2,1)} %slice_bitcast_fusion), calls=%async_computation.1 | async-start | bytes 524288 | tf_op jit(solution)/shard_map/all_to_all | solution.py:170
  149.7 5.8 %add_convert_fusion = bf16[2048,512]{0,1:T(8,128)(2,1)} fusion(bf16[2048,512]{1,0:T(8,128)(2,1)} %copy-done.19, bf16[1536,512]{1,0:T(8,128)(2,1)} %param.16, f32[2048,512]{0,1:T(8,128)} %copy.46, pred[2048]{0:T(1024)(128)(4,1)S(1)} %compare_and_fusion, bf16[2048,512]{0,1:T(8,128)(2,1)S(1)} %copy-done.5), kind=kOutput, calls=%fused_computation.7 | convolution fusion | flops 1078984704 | bytes 11012096 | tf_op jit(solution)/shard_map/dot_general | solution.py:54
  155.5 4.0 copy.50
  162.0 53.1 %all-reduce.7.cloned.1.call-done = (bf16[8,4,48,512]{3,2,1,0:T(8,128)(2,1)}, bf16[8,4,16,512]{3,2,1,0:T(8,128)(2,1)}, bf16[8,4,32,512]{3,2,1,0:T(8,128)(2,1)}, bf16[8,4,16,512]{3,2,1,0:T(8,128)(2,1)}) async-done(((bf16[8,4,48,512]{3,2,1,0:T(8,128)(2,1)}, bf16[8,4,16,512]{3,2,1,0:T(8,128)(2,1)}, bf16[8,4,32,512]{3,2,1,0:T(8,128)(2,1)}, bf16[8,4,16,512]{3,2,1,0:T(8,128)(2,1)}), ...) | async-done | bytes 3670032
  230.0 50.5 %reduce-scatter.19.cloned.1.call-done = bf16[1,1,16,512]{3,2,1,0:T(8,128)(2,1)} async-done(((bf16[8,1,16,512]{3,2,1,0:T(8,128)(2,1)}), bf16[1,1,16,512]{3,2,1,0:T(8,128)(2,1)}) %reduce-scatter.19.cloned.1.call-update) | async-done | bytes 16400 | tf_op jit(solution)/shard_map/reduce_scatter | solution.py:196
  281.8 63.0 %reduce-scatter.23.cloned.1.call-done = bf16[1,1,16,512]{3,2,1,0:T(8,128)(2,1)} async-done(((bf16[8,1,16,512]{3,2,1,0:T(8,128)(2,1)}), bf16[1,1,16,512]{3,2,1,0:T(8,128)(2,1)}) %reduce-scatter.23.cloned.1.call-update) | async-done | bytes 16400 | tf_op jit(solution)/shard_map/reduce_scatter | solution.py:196
  346.1 63.0 %reduce-scatter.21.cloned.1.call-done = bf16[1,1,32,512]{3,2,1,0:T(8,128)(2,1)} async-done(((bf16[8,1,32,512]{3,2,1,0:T(8,128)(2,1)}), bf16[1,1,32,512]{3,2,1,0:T(8,128)(2,1)}) %reduce-scatter.21.cloned.1.call-update) | async-done | bytes 32784 | tf_op jit(solution)/shard_map/reduce_scatter | solution.py:196
  410.4 62.9 %reduce-scatter.17.cloned.1.call-done = bf16[1,1,48,512]{3,2,1,0:T(8,128)(2,1)} async-done(((bf16[8,1,48,512]{3,2,1,0:T(8,128)(2,1)}), bf16[1,1,48,512]{3,2,1,0:T(8,128)(2,1)}) %reduce-scatter.17.cloned.1.call-update) | async-done | bytes 49168 | tf_op jit(solution)/shard_map/reduce_scatter | solution.py:196
  (177 shorter events, 77.7 us)
Async XLA Ops:
  7.2 69.7 %copy-start = (bf16[512,512]{1,0:T(8,128)(2,1)S(1)}, bf16[512,512]{1,0:T(8,128)(2,1)}, u32[]{:S(2)}) copy-start(bf16[512,512]{1,0:T(8,128)(2,1)} %param.17) | copy-start | bytes 1572868
  7.2 13.3 %copy-start.26 = (s32[1,32,8]{1,2,0:T(8,128)S(1)}, s32[1,32,8]{1,2,0:T(8,128)}, u32[]{:S(2)}) copy-start(s32[1,32,8]{1,2,0:T(8,128)} %param.23) | copy-start | bytes 3076
  7.2 13.3 %copy-start.1 = (bf16[256,512]{1,0:T(8,128)(2,1)S(1)}, bf16[256,512]{1,0:T(8,128)(2,1)}, u32[]{:S(2)}) copy-start(bf16[256,512]{1,0:T(8,128)(2,1)} %param.12) | copy-start | bytes 786436
  11.9 14.0 %copy-start.28 = (s32[2048]{0:T(1024)S(1)}, s32[2048]{0:T(1024)}, u32[]{:S(2)}) copy-start(s32[2048]{0:T(1024)} %param.21) | copy-start | bytes 24580
  12.6 13.3 %copy-start.27 = (s32[2048]{0:T(1024)S(1)}, s32[2048]{0:T(1024)}, u32[]{:S(2)}) copy-start(s32[2048]{0:T(1024)} %param.20) | copy-start | bytes 24580
  12.6 13.5 %copy-start.29 = (s32[1,4,64]{2,1,0:T(4,128)S(1)}, s32[1,4,64]{2,1,0:T(4,128)}, u32[]{:S(2)}) copy-start(s32[1,4,64]{2,1,0:T(4,128)} %param.22) | copy-start | bytes 3076
  12.6 13.6 %copy-start.11 = (bf16[1024,512]{1,0:T(8,128)(2,1)S(1)}, bf16[1024,512]{1,0:T(8,128)(2,1)}, u32[]{:S(2)}) copy-start(bf16[1024,512]{1,0:T(8,128)(2,1)} %param.18) | copy-start | bytes 3145732
  12.6 40.7 %collective-permute-start = (bf16[64,512]{1,0:T(8,128)(2,1)}, bf16[64,512]{1,0:T(8,128)(2,1)}, u32[]{:S(2)}, u32[]{:S(2)}) collective-permute-start(bf16[64,512]{1,0:T(8,128)(2,1)} %get-tuple-element.49), channel_id=1, source_target_pairs={{0,4},{4,8},{8,12},{12,16},{16,20},{20,24},{24,28},{28,0},{1,5},{5... | collective-permute-start | bytes 196616 | tf_op jit(solution)/shard_map/ppermute | solution.py:13
  15.7 38.5 %collective-permute-start.1 = (bf16[64,512]{1,0:T(8,128)(2,1)}, bf16[64,512]{1,0:T(8,128)(2,1)}, u32[]{:S(2)}, u32[]{:S(2)}) collective-permute-start(bf16[64,512]{1,0:T(8,128)(2,1)} %get-tuple-element.48), channel_id=1, source_target_pairs={{0,28},{4,0},{8,4},{12,8},{16,12},{20,16},{24,20},{28,24},{1,29},{... | collective-permute-start | bytes 196616 | tf_op jit(solution)/shard_map/ppermute | solution.py:13
  18.8 36.2 %collective-permute-start.2 = (bf16[64,512]{1,0:T(8,128)(2,1)}, bf16[64,512]{1,0:T(8,128)(2,1)}, u32[]{:S(2)}, u32[]{:S(2)}) collective-permute-start(bf16[64,512]{1,0:T(8,128)(2,1)} %get-tuple-element.47), channel_id=1, source_target_pairs={{0,1},{1,2},{2,3},{3,0},{4,5},{5,6},{6,7},{7,4},{8,9},{9,10},{10,1... | collective-permute-start | bytes 196616 | tf_op jit(solution)/shard_map/ppermute | solution.py:13
  18.8 37.1 %collective-permute-start.3 = (bf16[64,512]{1,0:T(8,128)(2,1)}, bf16[64,512]{1,0:T(8,128)(2,1)S(1)}, u32[]{:S(2)}, u32[]{:S(2)}) collective-permute-start(bf16[64,512]{1,0:T(8,128)(2,1)} %get-tuple-element.46), channel_id=1, source_target_pairs={{0,3},{1,0},{2,1},{3,2},{4,7},{5,4},{6,5},{7,6},{8,11},{9,8},{10,9... | collective-permute-start | bytes 196616 | tf_op jit(solution)/shard_map/ppermute | solution.py:13
  22.6 33.3 %all-to-all-start = ((bf16[32,8,512]{2,1,0:T(8,128)(2,1)}), bf16[32,8,512]{2,1,0:T(8,128)(2,1)S(1)}, u32[]{:S(2)}, u32[]{:S(2)}) async-start(bf16[32,8,512]{2,1,0:T(8,128)(2,1)} %bitcast_select_fusion), calls=%async_computation | async-start | bytes 524288 | tf_op jit(solution)/shard_map/all_to_all | solution.py:107
  25.8 189.2 %all-reduce.7.cloned.1.call-start = ((), (), s32[]{:S(2)}) async-start(), calls=%async_computation.10 | async-start | bytes 7340032
  26.0 43.2 %copy-start.30 = (pred[2048]{0:T(1024)(128)(4,1)}, pred[2048]{0:T(1024)(128)(4,1)S(1)}, u32[]{:S(2)}) copy-start(pred[2048]{0:T(1024)(128)(4,1)S(1)} %compare_and_fusion.1) | copy-start | bytes 6148
  106.7 5.9 %copy-start.4 = (f32[2048,512]{0,1:T(8,128)S(1)}, f32[2048,512]{0,1:T(8,128)}, u32[]{:S(2)}) copy-start(f32[2048,512]{0,1:T(8,128)} %copy.46) | copy-start | bytes 12582916
  137.3 84.0 %collective-permute-start.4 = (bf16[64,512]{1,0:T(8,128)(2,1)}, bf16[64,512]{1,0:T(8,128)(2,1)}, u32[]{:S(2)}, u32[]{:S(2)}) collective-permute-start(bf16[64,512]{1,0:T(8,128)(2,1)} %get-tuple-element.43), channel_id=1, source_target_pairs={{0,28},{4,0},{8,4},{12,8},{16,12},{20,16},{24,20},{28,24},{1,29},{... | collective-permute-start | bytes 196616 | tf_op jit(solution)/shard_map/ppermute | solution.py:13
  141.9 80.3 %collective-permute-start.5 = (bf16[64,512]{1,0:T(8,128)(2,1)}, bf16[64,512]{1,0:T(8,128)(2,1)}, u32[]{:S(2)}, u32[]{:S(2)}) collective-permute-start(bf16[64,512]{1,0:T(8,128)(2,1)} %get-tuple-element.42), channel_id=1, source_target_pairs={{0,4},{4,8},{8,12},{12,16},{16,20},{20,24},{24,28},{28,0},{1,5},{5... | collective-permute-start | bytes 196616 | tf_op jit(solution)/shard_map/ppermute | solution.py:13
  141.9 83.6 %collective-permute-start.6 = (bf16[64,512]{1,0:T(8,128)(2,1)}, bf16[64,512]{1,0:T(8,128)(2,1)S(1)}, u32[]{:S(2)}, u32[]{:S(2)}) collective-permute-start(bf16[64,512]{1,0:T(8,128)(2,1)} %get-tuple-element.41), channel_id=1, source_target_pairs={{0,3},{1,0},{2,1},{3,2},{4,7},{5,4},{6,5},{7,6},{8,11},{9,8},{10,9... | collective-permute-start | bytes 196616 | tf_op jit(solution)/shard_map/ppermute | solution.py:13
  142.8 82.7 %collective-permute-start.7 = (bf16[64,512]{1,0:T(8,128)(2,1)}, bf16[64,512]{1,0:T(8,128)(2,1)S(1)}, u32[]{:S(2)}, u32[]{:S(2)}) collective-permute-start(bf16[64,512]{1,0:T(8,128)(2,1)} %get-tuple-element.40), channel_id=1, source_target_pairs={{0,1},{1,2},{2,3},{3,0},{4,5},{5,6},{6,7},{7,4},{8,9},{9,10},{10,1... | collective-permute-start | bytes 196616 | tf_op jit(solution)/shard_map/ppermute | solution.py:13
  143.5 82.0 %all-to-all-start.1 = ((bf16[32,8,512]{2,1,0:T(8,128)(2,1)}), bf16[32,8,512]{2,1,0:T(8,128)(2,1)}, u32[]{:S(2)}, u32[]{:S(2)}) async-start(bf16[32,8,512]{2,1,0:T(8,128)(2,1)} %slice_bitcast_fusion), calls=%async_computation.1 | async-start | bytes 524288 | tf_op jit(solution)/shard_map/all_to_all | solution.py:170
  149.7 130.8 %reduce-scatter.19.cloned.1.call-start = ((), (), s32[]{:S(2)}) async-start(), calls=%async_computation.7 | async-start | bytes 147456 | tf_op jit(solution)/shard_map/reduce_scatter | solution.py:196
  217.3 127.4 %reduce-scatter.23.cloned.1.call-start = ((), (), s32[]{:S(2)}) async-start(), calls=%async_computation.9 | async-start | bytes 147456 | tf_op jit(solution)/shard_map/reduce_scatter | solution.py:196
  221.3 187.7 %reduce-scatter.21.cloned.1.call-start = ((), (), s32[]{:S(2)}) async-start(), calls=%async_computation.8 | async-start | bytes 294912 | tf_op jit(solution)/shard_map/reduce_scatter | solution.py:196
  225.4 248.0 %reduce-scatter.17.cloned.1.call-start = ((), (), s32[]{:S(2)}) async-start(), calls=%async_computation.6 | async-start | bytes 442368 | tf_op jit(solution)/shard_map/reduce_scatter | solution.py:196
  (26 other events, 68.5 us)
Sparse Core Ops, SparseCore 0:
  132.6 82.4 all-reduce.6
  218.4 61.9 reduce-scatter.18
  283.8 60.9 reduce-scatter.22
  347.9 61.0 reduce-scatter.20
  412.1 61.1 reduce-scatter.16
where the time goes:
time: 483 us; the launch traced here: 481 us
  waiting for transfers between devices  293 us (61%)
  local copies, waits for them, and re-layouts  84 us (17%)
  matrix products  46.9 us (10%)
  starting transfers between devices  23 us (5%)
  other arithmetic  20.7 us (4%)
  between operations  14.3 us (3%)
    reduce_scatter x4, waiting for transfers between devices, shards(): lax.psum_scatter(shortened(partial_sums), 'row', scatter_dimension=0, til...  239 us
    unnamed x6, waiting for transfers between devices  53.2 us
    unnamed x89, local copies, waits for them, and re-layouts  36.2 us
    dot_general x10, matrix products, plain_dot(): return jnp.dot(left, right, preferred_element_type=jnp.float32)  21.9 us
    gather x2, local copies, waits for them, and re-layouts, shards(): jnp.take(gathered_grad, receiver, axis=0)  14.4 us
    ppermute x8, starting transfers between devices, passed_along(): lax.ppermute(value, axis, [(i, (i + by) % peers) for i in range(peers)])  13.4 us
    gather x2, local copies, waits for them, and re-layouts, shards(): sent_rows = jnp.take(table, sender_code, axis=0)  13.3 us
    gather x2, local copies, waits for them, and re-layouts, shards(): recv_rows = jnp.take(node_latent, receiver, axis=0)  13.2 us
  transfers between devices with their start and end apart: 15, of which 5 were waited for; matrix products, arithmetic and copies ran while one was open for 14% of the time, Pallas kernels for 0%

commit v1 on v0

v1 whole, which is shorter than its diff:
```python
import functools
import math

import jax
import jax.numpy as jnp
from jax import lax
from jax.experimental import pallas as pl
from jax.experimental.pallas import tpu as pltpu
from jax.sharding import PartitionSpec as P

EPS = 1e-05
MESH = pl.DeviceIdType.MESH
F32 = jnp.float32
BF16 = jnp.bfloat16


def passed_along(value, axis, by):
    peers = lax.axis_size(axis)
    return lax.ppermute(value, axis, [(i, (i + by) % peers) for i in range(peers)])


def dot(left, right):
    return jnp.dot(left, right, preferred_element_type=F32)


def dot_t(left, weight):
    return lax.dot_general(left, weight, (((1,), (1,)), ((), ())), preferred_element_type=F32)


def cross(left, right):
    return lax.dot_general(left, right, (((0,), (0,)), ((), ())), preferred_element_type=F32)


def norm_parts(value):
    mean = jnp.mean(value, -1, keepdims=True)
    centred = value - mean
    recip = lax.rsqrt(jnp.mean(centred * centred, -1, keepdims=True) + EPS)
    return centred * recip, recip


def norm_back(normed, recip, grad):
    inner = (
        grad
        - jnp.mean(grad, -1, keepdims=True)
        - normed * jnp.mean(grad * normed, -1, keepdims=True)
    )
    return recip * inner


def row_hot(codes, count):
    tile = codes.shape[1]
    column = jnp.transpose(jnp.broadcast_to(codes, (128, tile)))
    lane = lax.broadcasted_iota(jnp.int32, (tile, 128), 1)
    groups = [
        jnp.where(column == lane + 128 * g, 1.0, 0.0).astype(BF16) for g in range(count // 128)
    ]
    return jnp.concatenate(groups, 1)


def col_hot(codes, count):
    tile = codes.shape[1]
    ids = lax.broadcasted_iota(jnp.int32, (count, tile), 0)
    return jnp.where(codes == ids, 1.0, 0.0).astype(BF16)


def compute_kernel(
    tile,
    edge_scale,
    node_scale,
    node_ref,
    edge_ref,
    ncot_ref,
    ecot_ref,
    w_in,
    w_out,
    v_in,
    v_out,
    code_ref,
    recv_ref,
    ext_ref,
    node_new_ref,
    edge_new_ref,
    part_ref,
    grad_edge_ref,
    ext_grad_ref,
    g_in_ref,
    g_out_ref,
    h_in_ref,
    h_out_ref,
    proj,
    slope,
    normed_s,
    recip_s,
    hidden_s,
    gath_s,
    gg_s,
    sums_s,
    acc_e,
    acc_o,
):
    nodes, width = node_ref.shape
    edges = edge_ref.shape[0]
    ext = ext_ref.shape[0]
    rows = nodes + ext
    steps = edges // tile
    w_e = w_in.at[pl.ds(0, width)]
    w_s = w_in.at[pl.ds(width, width)]
    w_r = w_in.at[pl.ds(2 * width, width)]
    v_a = v_in.at[pl.ds(0, width)]
    v_b = v_in.at[pl.ds(width, width)]
    proj[pl.ds(0, nodes), :] = dot(node_ref[...], w_s[...]).astype(BF16)
    proj[pl.ds(nodes, ext), :] = dot(ext_ref[...], w_s[...]).astype(BF16)
    proj[pl.ds(rows, nodes), :] = dot(node_ref[...], w_r[...]).astype(BF16)
    gath_s[...] = jnp.zeros_like(gath_s)

    def forward(step, carry):
        span = pl.ds(pl.multiple_of(step * tile, tile), tile)
        codes = code_ref[step]
        recvs = recv_ref[step]
        hot = jnp.concatenate([row_hot(codes, rows), row_hot(recvs, nodes)], 1)
        edge = edge_ref[span, :]
        pre = dot(edge, w_e[...]) + dot(hot, proj[...])
        sigma = jax.nn.sigmoid(pre)
        slope[span, :] = sigma * (1.0 + pre * (1.0 - sigma))
        hidden = (pre * sigma).astype(BF16)
        hidden_s[span, :] = hidden
        normed, recip = norm_parts(dot(hidden, w_out[...]))
        normed_s[span, :] = normed
        recip_s[span, :] = jnp.broadcast_to(recip, (tile, 128))
        new = (edge.astype(F32) + normed).astype(BF16)
        edge_new_ref[span, :] = new
        gath_s[...] += dot(col_hot(recvs, nodes), new)
        return carry

    lax.fori_loop(0, steps, forward, 0)

    node = node_ref[...]
    gathered = gath_s[...].astype(BF16)
    pre = dot(node, v_a[...]) + dot(gathered, v_b[...])
    sigma = jax.nn.sigmoid(pre)
    hidden = (pre * sigma).astype(BF16)
    normed, recip = norm_parts(dot(hidden, v_out[...]))
    node_new_ref[...] = (node.astype(F32) + normed).astype(BF16)
    ncot = ncot_ref[...].astype(F32)
    delta = norm_back(normed, recip, ncot).astype(BF16)
    pre_delta = (dot_t(delta, v_out[...]) * (sigma * (1.0 + pre * (1.0 - sigma)))).astype(BF16)
    gg_s[...] = dot_t(pre_delta, v_b[...]).astype(BF16)
    part_ref[...] = ncot + dot_t(pre_delta, v_a[...])
    h_in_ref[pl.ds(0, width), :] = (cross(node, pre_delta) * node_scale).astype(BF16)
    h_in_ref[pl.ds(width, width), :] = (cross(gathered, pre_delta) * node_scale).astype(BF16)
    h_out_ref[...] = (cross(hidden, delta) * node_scale).astype(BF16)

    sums_s[...] = jnp.zeros_like(sums_s)
    acc_e[...] = jnp.zeros_like(acc_e)
    acc_o[...] = jnp.zeros_like(acc_o)

    def backward(step, carry):
        span = pl.ds(pl.multiple_of(step * tile, tile), tile)
        codes = code_ref[step]
        recvs = recv_ref[step]
        total = ecot_ref[span, :].astype(F32) + dot(row_hot(recvs, nodes), gg_s[...])
        recip = recip_s[span, :][:, :1]
        delta = norm_back(normed_s[span, :], recip, total).astype(BF16)
        pre_delta = (dot_t(delta, w_out[...]) * slope[span, :]).astype(BF16)
        grad_edge_ref[span, :] = (total + dot_t(pre_delta, w_e[...])).astype(BF16)
        hot = jnp.concatenate([col_hot(codes, rows), col_hot(recvs, nodes)], 0)
        sums_s[...] += dot(hot, pre_delta)
        acc_e[...] += cross(edge_ref[span, :], pre_delta)
        acc_o[...] += cross(hidden_s[span, :], delta)
        return carry

    lax.fori_loop(0, steps, backward, 0)

    g_in_ref[pl.ds(0, width), :] = (acc_e[...] * edge_scale).astype(BF16)
    g_out_ref[...] = (acc_o[...] * edge_scale).astype(BF16)
    near = sums_s[pl.ds(0, nodes), :].astype(BF16)
    far = sums_s[pl.ds(nodes, ext), :].astype(BF16)
    recv = sums_s[pl.ds(rows, nodes), :].astype(BF16)
    ext_grad_ref[...] = dot_t(far, w_s[...]).astype(BF16)
    part_ref[...] += dot_t(near, w_s[...]) + dot_t(recv, w_r[...])
    g_in_ref[pl.ds(width, width), :] = (
        (cross(node_ref[...], near) + cross(ext_ref[...], far)) * edge_scale
    ).astype(BF16)
    g_in_ref[pl.ds(2 * width, width), :] = (cross(node_ref[...], recv) * edge_scale).astype(BF16)


def compute(node, edge, ncot, ecot, w_in, w_out, v_in, v_out, code, recv, ext, scales):
    nodes, width = node.shape
    edges = edge.shape[0]
    rows = nodes + ext.shape[0]
    tile = math.gcd(edges, 512)
    vmem = pl.BlockSpec(memory_space=pltpu.VMEM)
    shape = jax.ShapeDtypeStruct
    units = 2 * edges * width
    work = units * width * 5 + units * (2 * (rows + nodes) + 2 * nodes)
    return pl.pallas_call(
        functools.partial(compute_kernel, tile, *scales),
        name="processor",
        out_shape=(
            shape((nodes, width), BF16),
            shape((edges, width), BF16),
            shape((nodes, width), F32),
            shape((edges, width), BF16),
            shape(ext.shape, BF16),
            shape(w_in.shape, BF16),
            shape(w_out.shape, BF16),
            shape(v_in.shape, BF16),
            shape(v_out.shape, BF16),
        ),
        in_specs=[vmem] * 11,
        out_specs=[vmem] * 9,
        scratch_shapes=[
            pltpu.VMEM((rows + nodes, width), BF16),
            pltpu.VMEM((edges, width), F32),
            pltpu.VMEM((edges, width), F32),
            pltpu.VMEM((edges, 128), F32),
            pltpu.VMEM((edges, width), BF16),
            pltpu.VMEM((nodes, width), F32),
            pltpu.VMEM((nodes, width), BF16),
            pltpu.VMEM((rows + nodes, width), F32),
            pltpu.VMEM((width, width), F32),
            pltpu.VMEM((width, width), F32),
        ],
        compiler_params=pltpu.CompilerParams(vmem_limit_bytes=62 * 1024 * 1024),
        cost_estimate=pl.CostEstimate(flops=work, bytes_accessed=20 * units, transcendentals=units),
    )(
        node,
        edge,
        ncot,
        ecot,
        w_in,
        w_out,
        v_in,
        v_out,
        code.reshape(edges // tile, 1, tile),
        recv.reshape(edges // tile, 1, tile),
        ext,
    )


def bit_count(size):
    bits = size.bit_length() - 1
    assert size == 1 << bits
    return bits


def scatter_kernel(orders, row_bits, col_bits, count, *refs):
    bits = row_bits + col_bits
    inputs = refs[:count]
    outputs = refs[count : 2 * count]
    recv = [refs[2 * count + a * bits : 2 * count + (a + 1) * bits] for a in range(count)]
    at = 2 * count + count * bits
    held = [refs[at + a * (bits - 1) : at + (a + 1) * (bits - 1)] for a in range(count)]
    send_sem, recv_sem = refs[-2:]
    row = lax.axis_index("row")
    col = lax.axis_index("col")

    def mine(bit):
        if bit < row_bits:
            return (row // (1 << (row_bits - 1 - bit))) % 2
        return (col // (1 << (bits - 1 - bit))) % 2

    def partner(bit):
        if bit < row_bits:
            step = 1 << (row_bits - 1 - bit)
            return (row + step * (1 - 2 * mine(bit)), col)
        step = 1 << (bits - 1 - bit)
        return (row, col + step * (1 - 2 * mine(bit)))

    barrier = pltpu.get_barrier_semaphore()
    for bit in range(bits):
        pl.semaphore_signal(barrier, inc=1, device_id=partner(bit), device_id_type=MESH)
    pl.semaphore_wait(barrier, bits)

    left = [list(range(bits)) for _ in range(count)]
    current = list(inputs)

    def copy_of(a, phase):
        bit = orders[a][phase]
        place = left[a].index(bit)
        spot = (slice(None),) * place + (1 - mine(bit),)
        return pltpu.make_async_remote_copy(
            src_ref=current[a].at[spot],
            dst_ref=recv[a][phase],
            send_sem=send_sem.at[a, phase],
            recv_sem=recv_sem.at[a, phase],
            device_id=partner(bit),
            device_id_type=MESH,
        )

    copies = [copy_of(a, 0) for a in range(count)]
    for item in copies:
        item.start()
    sent = []
    for phase in range(bits):
        for a in range(count):
            copies[a].wait_recv()
            sent.append(copies[a])
            bit = orders[a][phase]
            place = left[a].index(bit)
            spot = (slice(None),) * place + (mine(bit),)
            value = current[a][spot].astype(F32) + recv[a][phase][...].astype(F32)
            left[a].remove(bit)
            if phase == bits - 1:
                outputs[a][...] = value
            else:
                held[a][phase][...] = value.astype(BF16)
                current[a] = held[a][phase]
                copies[a] = copy_of(a, phase + 1)
                copies[a].start()
    for item in sent:
        item.wait_send()


def scatter_sum(grads):
    rows_grid = lax.axis_size("row")
    cols_grid = lax.axis_size("col")
    row_bits = bit_count(rows_grid)
    col_bits = bit_count(cols_grid)
    bits = row_bits + col_bits
    peers = rows_grid * cols_grid
    width = grads[0].shape[-1]
    slabs = [g.shape[0] // peers for g in grads]
    shaped = [g.reshape((2,) * bits + (s, width)) for g, s in zip(grads, slabs)]
    core = bits - 1
    along_col = list(range(bits - 2, row_bits - 1, -1))
    row_near = [row_bits - 1]
    row_far = list(range(row_bits - 2, -1, -1))
    turns = [
        [core] + along_col + row_near + row_far,
        [core] + row_near + row_far + along_col,
        [core] + row_far + along_col + row_near,
        [core] + row_far + along_col + row_near,
    ]
    count = len(grads)
    vmem = pl.BlockSpec(memory_space=pltpu.VMEM)
    recv = [
        pltpu.VMEM((2,) * (bits - 1 - phase) + (s, width), BF16)
        for s in slabs
        for phase in range(bits)
    ]
    held = [
        pltpu.VMEM((2,) * (bits - 1 - phase) + (s, width), BF16)
        for s in slabs
        for phase in range(bits - 1)
    ]
    return pl.pallas_call(
        functools.partial(scatter_kernel, turns, row_bits, col_bits, count),
        name="scatter_sum",
        out_shape=tuple(jax.ShapeDtypeStruct((s, width), F32) for s in slabs),
        in_specs=[vmem] * count,
        out_specs=[vmem] * count,
        scratch_shapes=recv
        + held
        + [pltpu.SemaphoreType.DMA((count, bits)), pltpu.SemaphoreType.DMA((count, bits))],
        compiler_params=pltpu.CompilerParams(
            collective_id=0, has_side_effects=True, vmem_limit_bytes=40 * 1024 * 1024
        ),
        cost_estimate=pl.CostEstimate(flops=10**9, bytes_accessed=10**8, transcendentals=0),
    )(*shaped)


def shards(
    node_latent,
    edge_latent,
    node_cotangent,
    edge_cotangent,
    w_edge_in,
    w_edge_out,
    w_node_in,
    w_node_out,
    sender_code,
    receiver,
    near_list,
    far_list,
):
    node_rows, width = node_latent.shape
    edge_rows = edge_latent.shape[0]
    peers = lax.axis_size("row") * lax.axis_size("col")
    near_width = near_list.shape[2]
    far_width = far_list.shape[2]
    near_rows = 4 * near_width
    moves = (("row", 1), ("row", -1), ("col", 1), ("col", -1))
    owner = jnp.concatenate([near_list.reshape(-1), far_list.reshape(-1)], 0)
    node_ids = jnp.arange(node_rows, dtype=jnp.int32)
    offered = dot((owner[:, None] == node_ids[None, :]).astype(BF16), node_latent).astype(BF16)
    parts = []
    for slot, (axis, by) in enumerate(moves):
        parts.append(
            passed_along(offered[slot * near_width : (slot + 1) * near_width], axis, by)
        )
    far_send = offered[near_rows:].reshape(peers, far_width, width)
    far_recv = lax.all_to_all(far_send, ("row", "col"), split_axis=0, concat_axis=0, tiled=True)
    ext = jnp.concatenate(parts + [far_recv.reshape(peers * far_width, width)], 0)
    scales = (1.0 / math.sqrt(edge_rows * peers), 1.0 / math.sqrt(node_rows * peers))
    node_new, edge_new, part, grad_edge, ext_grad, g_in, g_out, h_in, h_out = compute(
        node_latent,
        edge_latent,
        node_cotangent,
        edge_cotangent,
        w_edge_in,
        w_edge_out,
        w_node_in,
        w_node_out,
        sender_code,
        receiver,
        ext,
        scales,
    )
    back = []
    for slot, (axis, by) in enumerate(moves):
        back.append(
            passed_along(ext_grad[slot * near_width : (slot + 1) * near_width], axis, -by)
        )
    far_back = lax.all_to_all(
        ext_grad[near_rows:].reshape(peers, far_width, width),
        ("row", "col"),
        split_axis=0,
        concat_axis=0,
        tiled=True,
    )
    returned = jnp.concatenate(back + [far_back.reshape(peers * far_width, width)], 0)
    owner_hot = (node_ids[:, None] == owner[None, :]).astype(BF16)
    grad_node = (part + dot(owner_hot, returned)).astype(BF16)
    s_in, s_hin, s_out, s_hout = scatter_sum((g_in, h_in, g_out, h_out))
    return (node_new, edge_new, grad_node, grad_edge, s_in, s_out, s_hin, s_hout)


def solution(mesh):
    both = ("row", "col")
    in_specs = (
        P(both, None),
        P(both, None),
        P(both, None),
        P(both, None),
        P(),
        P(),
        P(),
        P(),
        P(both),
        P(both),
        P(both, None, None),
        P(both, None, None),
    )
    out_specs = (P(both, None),) * 8
    return jax.shard_map(shards, mesh=mesh, in_specs=in_specs, out_specs=out_specs, check_vma=False)
```

time: 483 us -> 107 us (0.22)
  waiting for transfers between devices: 293 us -> 10.5 us
  local copies, waits for them, and re-layouts: 84 us -> 13.1 us
  Pallas kernels: 0 us -> 54.9 us
  matrix products: 46.9 us -> 1.61 us
  other arithmetic: 20.7 us -> 0.79 us
  between operations: 14.3 us -> 0.81 us
    reduce_scatter x4 -> x0, waiting for transfers between devices: 239 us -> none  [shards(): lax.psum_scatter(shortened(partial_sums), 'row', scatter_dimension=0, til...]
    pallas_call x0 -> x2, Pallas kernels: none -> 54.9 us  [the longest x1 28.7 us: scatter_sum(): pl.pallas_call(functools.partial(scatter_kernel, turns, row_bits, col_bit...]
    unnamed x6 -> x0, waiting for transfers between devices: 53.2 us -> none
    dot_general x25 -> x2, matrix products: 46.9 us -> 1.61 us  [dot(): return jnp.dot(left, right, preferred_element_type=F32)]
    gather x8 -> x0, local copies, waits for them, and re-layouts: 44.2 us -> none  [the longest x2 14.4 us: shards(): jnp.take(gathered_grad, receiver, axis=0)]
    unnamed x89 -> x26, local copies, waits for them, and re-layouts: 36.2 us -> 8.83 us
    ppermute x8, waiting for transfers between devices: 0.02 us -> 7.97 us  [passed_along(): lax.ppermute(value, axis, [(i, (i + by) % peers) for i in range(peers)])]
    reduce_sum x4 -> x0, other arithmetic: 5.85 us -> none  [the longest x2 5.12 us: norm_grad(): jnp.mean(grad, -1, keepdims=True)]
  transfers between devices with their start and end apart: 15 -> 10, of which waited for: 5 -> 3; matrix products, arithmetic and copies ran while one was open for 14% -> 1% of each run, Pallas kernels for 0% -> 27%
where the time goes in v1:
time: 107 us; the launch traced here: 106 us
  Pallas kernels  54.9 us (51%)
  starting transfers between devices  24.6 us (23%)
  local copies, waits for them, and re-layouts  13.1 us (12%)
  waiting for transfers between devices  10.5 us (10%)
  matrix products  1.61 us (2%)
    pallas_call x1, Pallas kernels, scatter_sum(): pl.pallas_call(functools.partial(scatter_kernel, turns, row_bits, col_bit...  28.7 us
    pallas_call x1, Pallas kernels, compute(): pl.pallas_call(functools.partial(compute_kernel, tile, *scales), name='pr...  26.2 us
    ppermute x8, starting transfers between devices, passed_along(): lax.ppermute(value, axis, [(i, (i + by) % peers) for i in range(peers)])  16.4 us
    unnamed x26, local copies, waits for them, and re-layouts  8.83 us
    ppermute x8, waiting for transfers between devices, passed_along(): lax.ppermute(value, axis, [(i, (i + by) % peers) for i in range(peers)])  7.97 us
    all_to_all x1, starting transfers between devices, shards(): lax.all_to_all(far_send, ('row', 'col'), split_axis=0, concat_axis=0, til...  4.89 us
    all_to_all x1, starting transfers between devices, shards(): lax.all_to_all(ext_grad[near_rows:].reshape(peers, far_width, width), ('r...  3.28 us
    all_to_all x1, waiting for transfers between devices, shards(): lax.all_to_all(far_send, ('row', 'col'), split_axis=0, concat_axis=0, til...  2.53 us
  transfers between devices with their start and end apart: 10, of which 3 were waited for; matrix products, arithmetic and copies ran while one was open for 1% of the time, Pallas kernels for 27%

profile of v1, /device:TPU:0, one launch (start us, length us, event | category | flops | bytes accessed | tf_op | source)
XLA Modules:
  0.0 106.3 jit_solution(3347118941891207866)
XLA Ops:
  0.6 0.8 reshape.56
  1.4 0.8 copy.20
  2.3 1.3 %convolution_convert_fusion = bf16[512,512]{1,0:T(8,128)(2,1)S(1)} fusion(bf16[256,512]{1,0:T(8,128)(2,1)} %node_ref.1, s32[512]{0:T(512)S(1)} %constant_dynamic-update-slice_fusion.9), kind=kOutput, calls=%fused_computation | convolution fusion | flops 134610944 | bytes 788480 | tf_op jit(solution)/shard_map/dot_general | solution.py:23
  3.6 3.0 %collective-permute-start = (bf16[64,512]{1,0:T(8,128)(2,1)S(1)}, bf16[64,512]{1,0:T(8,128)(2,1)S(1)}, u32[]{:S(2)}, u32[]{:S(2)}) collective-permute-start(bf16[64,512]{1,0:T(8,128)(2,1)S(1)} %get-tuple-element.41), channel_id=1, source_target_pairs={{0,4},{4,8},{8,12},{12,16},{16,20},{20,24},{24,28},{28,0},{1,5},{5... | collective-permute-start | bytes 196616 | tf_op jit(solution)/shard_map/ppermute | solution.py:19
  7.4 4.9 %all-to-all-start = ((bf16[32,8,512]{2,1,0:T(8,128)(2,1)}), bf16[32,8,512]{2,1,0:T(8,128)(2,1)S(1)}, u32[]{:S(2)}, u32[]{:S(2)}) async-start(bf16[32,8,512]{2,1,0:T(8,128)(2,1)} %slice_bitcast_fusion), calls=%async_computation | async-start | bytes 524288 | tf_op jit(solution)/shard_map/all_to_all | solution.py:393
  12.3 1.5 %collective-permute-start.3 = (bf16[64,512]{1,0:T(8,128)(2,1)S(1)}, bf16[64,512]{1,0:T(8,128)(2,1)S(1)}, u32[]{:S(2)}, u32[]{:S(2)}) collective-permute-start(bf16[64,512]{1,0:T(8,128)(2,1)S(1)} %get-tuple-element.38), channel_id=1, source_target_pairs={{0,3},{1,0},{2,1},{3,2},{4,7},{5,4},{6,5},{7,6},{8,11},{9,8},{10,9... | collective-permute-start | bytes 196616 | tf_op jit(solution)/shard_map/ppermute | solution.py:19
  13.8 4.3 %collective-permute-start.1 = (bf16[64,512]{1,0:T(8,128)(2,1)S(1)}, bf16[64,512]{1,0:T(8,128)(2,1)S(1)}, u32[]{:S(2)}, u32[]{:S(2)}) collective-permute-start(bf16[64,512]{1,0:T(8,128)(2,1)S(1)} %get-tuple-element.40), channel_id=1, source_target_pairs={{0,28},{4,0},{8,4},{12,8},{16,12},{20,16},{24,20},{28,24},{1,29},{... | collective-permute-start | bytes 196616 | tf_op jit(solution)/shard_map/ppermute | solution.py:19
  18.1 2.2 %collective-permute-done.1 = bf16[64,512]{1,0:T(8,128)(2,1)S(1)} collective-permute-done((bf16[64,512]{1,0:T(8,128)(2,1)S(1)}, bf16[64,512]{1,0:T(8,128)(2,1)S(1)}, u32[]{:S(2)}, u32[]{:S(2)}) %collective-permute-start.1) | collective-permute-done | bytes 65568 | tf_op jit(solution)/shard_map/ppermute | solution.py:19
  20.3 2.5 %all-to-all-done = bf16[32,8,512]{2,1,0:T(8,128)(2,1)S(1)} async-done(((bf16[32,8,512]{2,1,0:T(8,128)(2,1)}), bf16[32,8,512]{2,1,0:T(8,128)(2,1)S(1)}, u32[]{:S(2)}, u32[]{:S(2)}) %all-to-all-start) | async-done | bytes 262176 | tf_op jit(solution)/shard_map/all_to_all | solution.py:393
  22.9 0.8 copy-done.5
  23.7 26.2 %processor.1 = (bf16[256,512]{1,0:T(8,128)(2,1)}, bf16[2048,512]{1,0:T(8,128)(2,1)}, f32[256,512]{1,0:T(8,128)}, bf16[2048,512]{1,0:T(8,128)(2,1)}, bf16[512,512...) custom-call(bf16[256,512]{1,0:T(8,128)(2,1)} %node_ref.1, ...), custom_call_target="tpu_custom_call" | custom-call | flops 10737418240 | bytes 41943040 | tf_op jit(solution)/shard_map/processor/pallas_call | solution.py:196
  49.9 1.7 %slice_bitcast_fusion.1 = bf16[32,8,512]{2,1,0:T(8,128)(2,1)} fusion(bf16[512,512]{1,0:T(8,128)(2,1)} %get-tuple-element.24), kind=kLoop, calls=%fused_computation.8 | loop fusion | bytes 524288 | tf_op jit(solution)/shard_map/reshape | solution.py:416
  51.5 1.0 fusion.3
  52.5 3.3 %all-to-all-start.1 = ((bf16[32,8,512]{2,1,0:T(8,128)(2,1)}), bf16[32,8,512]{2,1,0:T(8,128)(2,1)S(1)}, u32[]{:S(2)}, u32[]{:S(2)}) async-start(bf16[32,8,512]{2,1,0:T(8,128)(2,1)} %slice_bitcast_fusion.1), calls=%async_computation.1 | async-start | bytes 524288 | tf_op jit(solution)/shard_map/all_to_all | solution.py:415
  55.8 4.6 %collective-permute-start.4 = (bf16[64,512]{1,0:T(8,128)(2,1)S(1)}, bf16[64,512]{1,0:T(8,128)(2,1)S(1)}, u32[]{:S(2)}, u32[]{:S(2)}) collective-permute-start(bf16[64,512]{1,0:T(8,128)(2,1)S(1)} %get-tuple-element.37), channel_id=1, source_target_pairs={{0,28},{4,0},{8,4},{12,8},{16,12},{20,16},{24,20},{28,24},{1,29},{... | collective-permute-start | bytes 196616 | tf_op jit(solution)/shard_map/ppermute | solution.py:19
  60.4 1.4 %copy-done = bf16[1536,512]{1,0:T(8,128)(2,1)S(1)} copy-done((bf16[1536,512]{1,0:T(8,128)(2,1)S(1)}, bf16[1536,512]{1,0:T(8,128)(2,1)}, u32[]{:S(2)}) %copy-start) | copy-done | bytes 1572888
  61.8 1.2 %copy-done.1 = bf16[1024,512]{1,0:T(8,128)(2,1)S(1)} copy-done((bf16[1024,512]{1,0:T(8,128)(2,1)S(1)}, bf16[1024,512]{1,0:T(8,128)(2,1)}, u32[]{:S(2)}) %copy-start.1) | copy-done | bytes 1048600
  63.0 1.0 copy-done.2
  64.1 1.0 copy-done.3
  65.1 28.7 %scatter_sum.1 = (f32[48,512]{1,0:T(8,128)S(1)}, f32[32,512]{1,0:T(8,128)S(1)}, f32[16,512]{1,0:T(8,128)S(1)}, f32[16,512]{1,0:T(8,128)S(1)}) custom-call(bf16[2,2,2,2,2,48,512]{6,5,4,3,2,1,0:T(8,128)(2,1)S(1)} %bitcast.16, bf16[2,2,2,2,2,32,512]{6,5,4,3,2,1,0:T(8,128)(2,1)S(1)} %bitcast.17, bf16[2,2,2,2,2,16,512]{6,5,4,3,2,1,0:T(8,128)(2,1)S(1)} %bitcast.18, ...), custom_call_target="tpu_custom_call" | custom-call | flops 1000000000 | bytes 100000000 | tf_op jit(solution)/shard_map/scatter_sum/pallas_call | solution.py:347
  93.9 1.7 %collective-permute-start.6 = (bf16[64,512]{1,0:T(8,128)(2,1)S(1)}, bf16[64,512]{1,0:T(8,128)(2,1)S(1)}, u32[]{:S(2)}, u32[]{:S(2)}) collective-permute-start(bf16[64,512]{1,0:T(8,128)(2,1)S(1)} %get-tuple-element.35), channel_id=1, source_target_pairs={{0,3},{1,0},{2,1},{3,2},{4,7},{5,4},{6,5},{7,6},{8,11},{9,8},{10,9... | collective-permute-start | bytes 196616 | tf_op jit(solution)/shard_map/ppermute | solution.py:19
  95.6 1.2 %collective-permute-start.5 = (bf16[64,512]{1,0:T(8,128)(2,1)S(1)}, bf16[64,512]{1,0:T(8,128)(2,1)S(1)}, u32[]{:S(2)}, u32[]{:S(2)}) collective-permute-start(bf16[64,512]{1,0:T(8,128)(2,1)S(1)} %get-tuple-element.36), channel_id=1, source_target_pairs={{0,4},{4,8},{8,12},{12,16},{16,20},{20,24},{24,28},{28,0},{1,5},{5... | collective-permute-start | bytes 196616 | tf_op jit(solution)/shard_map/ppermute | solution.py:19
  96.8 5.8 %collective-permute-done.5 = bf16[64,512]{1,0:T(8,128)(2,1)S(1)} collective-permute-done((bf16[64,512]{1,0:T(8,128)(2,1)S(1)}, bf16[64,512]{1,0:T(8,128)(2,1)S(1)}, u32[]{:S(2)}, u32[]{:S(2)}) %collective-permute-start.5) | collective-permute-done | bytes 65568 | tf_op jit(solution)/shard_map/ppermute | solution.py:19
  103.0 0.8 add_convert_fusion
  (37 shorter events, 3.8 us)
Async XLA Ops:
  3.6 14.5 %collective-permute-start = (bf16[64,512]{1,0:T(8,128)(2,1)S(1)}, bf16[64,512]{1,0:T(8,128)(2,1)S(1)}, u32[]{:S(2)}, u32[]{:S(2)}) collective-permute-start(bf16[64,512]{1,0:T(8,128)(2,1)S(1)} %get-tuple-element.41), channel_id=1, source_target_pairs={{0,4},{4,8},{8,12},{12,16},{16,20},{20,24},{24,28},{28,0},{1,5},{5... | collective-permute-start | bytes 196616 | tf_op jit(solution)/shard_map/ppermute | solution.py:19
  7.4 15.5 %all-to-all-start = ((bf16[32,8,512]{2,1,0:T(8,128)(2,1)}), bf16[32,8,512]{2,1,0:T(8,128)(2,1)S(1)}, u32[]{:S(2)}, u32[]{:S(2)}) async-start(bf16[32,8,512]{2,1,0:T(8,128)(2,1)} %slice_bitcast_fusion), calls=%async_computation | async-start | bytes 524288 | tf_op jit(solution)/shard_map/all_to_all | solution.py:393
  12.3 8.0 %collective-permute-start.3 = (bf16[64,512]{1,0:T(8,128)(2,1)S(1)}, bf16[64,512]{1,0:T(8,128)(2,1)S(1)}, u32[]{:S(2)}, u32[]{:S(2)}) collective-permute-start(bf16[64,512]{1,0:T(8,128)(2,1)S(1)} %get-tuple-element.38), channel_id=1, source_target_pairs={{0,3},{1,0},{2,1},{3,2},{4,7},{5,4},{6,5},{7,6},{8,11},{9,8},{10,9... | collective-permute-start | bytes 196616 | tf_op jit(solution)/shard_map/ppermute | solution.py:19
  13.8 6.5 %collective-permute-start.2 = (bf16[64,512]{1,0:T(8,128)(2,1)S(1)}, bf16[64,512]{1,0:T(8,128)(2,1)S(1)}, u32[]{:S(2)}, u32[]{:S(2)}) collective-permute-start(bf16[64,512]{1,0:T(8,128)(2,1)S(1)} %get-tuple-element.39), channel_id=1, source_target_pairs={{0,1},{1,2},{2,3},{3,0},{4,5},{5,6},{6,7},{7,4},{8,9},{9,10},{10,1... | collective-permute-start | bytes 196616 | tf_op jit(solution)/shard_map/ppermute | solution.py:19
  13.8 6.4 %collective-permute-start.1 = (bf16[64,512]{1,0:T(8,128)(2,1)S(1)}, bf16[64,512]{1,0:T(8,128)(2,1)S(1)}, u32[]{:S(2)}, u32[]{:S(2)}) collective-permute-start(bf16[64,512]{1,0:T(8,128)(2,1)S(1)} %get-tuple-element.40), channel_id=1, source_target_pairs={{0,28},{4,0},{8,4},{12,8},{16,12},{20,16},{24,20},{28,24},{1,29},{... | collective-permute-start | bytes 196616 | tf_op jit(solution)/shard_map/ppermute | solution.py:19
  22.9 0.8 copy-start.5
  52.5 50.2 %all-to-all-start.1 = ((bf16[32,8,512]{2,1,0:T(8,128)(2,1)}), bf16[32,8,512]{2,1,0:T(8,128)(2,1)S(1)}, u32[]{:S(2)}, u32[]{:S(2)}) async-start(bf16[32,8,512]{2,1,0:T(8,128)(2,1)} %slice_bitcast_fusion.1), calls=%async_computation.1 | async-start | bytes 524288 | tf_op jit(solution)/shard_map/all_to_all | solution.py:415
  55.8 41.0 %collective-permute-start.4 = (bf16[64,512]{1,0:T(8,128)(2,1)S(1)}, bf16[64,512]{1,0:T(8,128)(2,1)S(1)}, u32[]{:S(2)}, u32[]{:S(2)}) collective-permute-start(bf16[64,512]{1,0:T(8,128)(2,1)S(1)} %get-tuple-element.37), channel_id=1, source_target_pairs={{0,28},{4,0},{8,4},{12,8},{16,12},{20,16},{24,20},{28,24},{1,29},{... | collective-permute-start | bytes 196616 | tf_op jit(solution)/shard_map/ppermute | solution.py:19
  60.4 1.4 %copy-start = (bf16[1536,512]{1,0:T(8,128)(2,1)S(1)}, bf16[1536,512]{1,0:T(8,128)(2,1)}, u32[]{:S(2)}) copy-start(bf16[1536,512]{1,0:T(8,128)(2,1)} %get-tuple-element.26) | copy-start | bytes 4718596
  61.8 1.2 %copy-start.1 = (bf16[1024,512]{1,0:T(8,128)(2,1)S(1)}, bf16[1024,512]{1,0:T(8,128)(2,1)}, u32[]{:S(2)}) copy-start(bf16[1024,512]{1,0:T(8,128)(2,1)} %get-tuple-element.27) | copy-start | bytes 3145732
  63.0 1.0 copy-start.2
  64.1 1.0 copy-start.3
  65.1 37.9 %copy-start.4 = (f32[256,512]{1,0:T(8,128)S(1)}, f32[256,512]{1,0:T(8,128)}, u32[]{:S(2)}) copy-start(f32[256,512]{1,0:T(8,128)} %get-tuple-element.23) | copy-start | bytes 1572868
  93.8 8.8 %collective-permute-start.7 = (bf16[64,512]{1,0:T(8,128)(2,1)S(1)}, bf16[64,512]{1,0:T(8,128)(2,1)S(1)}, u32[]{:S(2)}, u32[]{:S(2)}) collective-permute-start(bf16[64,512]{1,0:T(8,128)(2,1)S(1)} %get-tuple-element.34), channel_id=1, source_target_pairs={{0,1},{1,2},{2,3},{3,0},{4,5},{5,6},{6,7},{7,4},{8,9},{9,10},{10,1... | collective-permute-start | bytes 196616 | tf_op jit(solution)/shard_map/ppermute | solution.py:19
  93.9 8.7 %collective-permute-start.6 = (bf16[64,512]{1,0:T(8,128)(2,1)S(1)}, bf16[64,512]{1,0:T(8,128)(2,1)S(1)}, u32[]{:S(2)}, u32[]{:S(2)}) collective-permute-start(bf16[64,512]{1,0:T(8,128)(2,1)S(1)} %get-tuple-element.35), channel_id=1, source_target_pairs={{0,3},{1,0},{2,1},{3,2},{4,7},{5,4},{6,5},{7,6},{8,11},{9,8},{10,9... | collective-permute-start | bytes 196616 | tf_op jit(solution)/shard_map/ppermute | solution.py:19
  95.6 7.0 %collective-permute-start.5 = (bf16[64,512]{1,0:T(8,128)(2,1)S(1)}, bf16[64,512]{1,0:T(8,128)(2,1)S(1)}, u32[]{:S(2)}, u32[]{:S(2)}) collective-permute-start(bf16[64,512]{1,0:T(8,128)(2,1)S(1)} %get-tuple-element.36), channel_id=1, source_target_pairs={{0,4},{4,8},{8,12},{12,16},{16,20},{20,24},{24,28},{28,0},{1,5},{5... | collective-permute-start | bytes 196616 | tf_op jit(solution)/shard_map/ppermute | solution.py:19

commit v2 on v1

--- a/solution.py
+++ b/solution.py
@@ -12,11 +12,6 @@
 MESH = pl.DeviceIdType.MESH
 F32 = jnp.float32
 BF16 = jnp.bfloat16
-
-
-def passed_along(value, axis, by):
-    peers = lax.axis_size(axis)
-    return lax.ppermute(value, axis, [(i, (i + by) % peers) for i in range(peers)])
 
 
 def dot(left, right):
@@ -77,12 +72,14 @@
     v_out,
     code_ref,
     recv_ref,
-    ext_ref,
+    near_ref,
+    far_ref,
     node_new_ref,
     edge_new_ref,
     part_ref,
     grad_edge_ref,
-    ext_grad_ref,
+    near_grad_ref,
+    far_grad_ref,
     g_in_ref,
     g_out_ref,
     h_in_ref,
@@ -100,8 +97,9 @@
 ):
     nodes, width = node_ref.shape
     edges = edge_ref.shape[0]
-    ext = ext_ref.shape[0]
-    rows = nodes + ext
+    near = near_ref.shape[0]
+    far = far_ref.shape[0]
+    rows = nodes + near + far
     steps = edges // tile
     w_e = w_in.at[pl.ds(0, width)]
     w_s = w_in.at[pl.ds(width, width)]
@@ -109,7 +107,8 @@
     v_a = v_in.at[pl.ds(0, width)]
     v_b = v_in.at[pl.ds(width, width)]
     proj[pl.ds(0, nodes), :] = dot(node_ref[...], w_s[...]).astype(BF16)
-    proj[pl.ds(nodes, ext), :] = dot(ext_ref[...], w_s[...]).astype(BF16)
+    proj[pl.ds(nodes, near), :] = dot(near_ref[...], w_s[...]).astype(BF16)
+    proj[pl.ds(nodes + near, far), :] = dot(far_ref[...], w_s[...]).astype(BF16)
     proj[pl.ds(rows, nodes), :] = dot(node_ref[...], w_r[...]).astype(BF16)
     gath_s[...] = jnp.zeros_like(gath_s)
 
@@ -173,21 +172,23 @@
 
     g_in_ref[pl.ds(0, width), :] = (acc_e[...] * edge_scale).astype(BF16)
     g_out_ref[...] = (acc_o[...] * edge_scale).astype(BF16)
-    near = sums_s[pl.ds(0, nodes), :].astype(BF16)
-    far = sums_s[pl.ds(nodes, ext), :].astype(BF16)
-    recv = sums_s[pl.ds(rows, nodes), :].astype(BF16)
-    ext_grad_ref[...] = dot_t(far, w_s[...]).astype(BF16)
-    part_ref[...] += dot_t(near, w_s[...]) + dot_t(recv, w_r[...])
-    g_in_ref[pl.ds(width, width), :] = (
-        (cross(node_ref[...], near) + cross(ext_ref[...], far)) * edge_scale
-    ).astype(BF16)
-    g_in_ref[pl.ds(2 * width, width), :] = (cross(node_ref[...], recv) * edge_scale).astype(BF16)
-
-
-def compute(node, edge, ncot, ecot, w_in, w_out, v_in, v_out, code, recv, ext, scales):
+    own_sum = sums_s[pl.ds(0, nodes), :].astype(BF16)
+    near_sum = sums_s[pl.ds(nodes, near), :].astype(BF16)
+    far_sum = sums_s[pl.ds(nodes + near, far), :].astype(BF16)
+    recv_sum = sums_s[pl.ds(rows, nodes), :].astype(BF16)
+    near_grad_ref[...] = dot_t(near_sum, w_s[...]).astype(BF16)
+    far_grad_ref[...] = dot_t(far_sum, w_s[...]).astype(BF16)
+    part_ref[...] += dot_t(own_sum, w_s[...]) + dot_t(recv_sum, w_r[...])
+    sent = cross(node_ref[...], own_sum) + cross(near_ref[...], near_sum)
+    sent += cross(far_ref[...], far_sum)
+    g_in_ref[pl.ds(width, width), :] = (sent * edge_scale).astype(BF16)
+    g_in_ref[pl.ds(2 * width, width), :] = (cross(node_ref[...], recv_sum) * edge_scale).astype(BF16)
+
+
+def compute(node, edge, ncot, ecot, w_in, w_out, v_in, v_out, code, recv, near, far, scales):
     nodes, width = node.shape
     edges = edge.shape[0]
-    rows = nodes + ext.shape[0]
+    rows = nodes + near.shape[0] + far.shape[0]
     tile = math.gcd(edges, 512)
     vmem = pl.BlockSpec(memory_space=pltpu.VMEM)
     shape = jax.ShapeDtypeStruct
@@ -201,14 +202,15 @@
             shape((edges, width), BF16),
             shape((nodes, width), F32),
             shape((edges, width), BF16),
-            shape(ext.shape, BF16),
+            shape(near.shape, BF16),
+            shape(far.shape, BF16),
             shape(w_in.shape, BF16),
             shape(w_out.shape, BF16),
             shape(v_in.shape, BF16),
             shape(v_out.shape, BF16),
         ),
-        in_specs=[vmem] * 11,
-        out_specs=[vmem] * 9,
+        in_specs=[vmem] * 12,
+        out_specs=[vmem] * 10,
         scratch_shapes=[
             pltpu.VMEM((rows + nodes, width), BF16),
             pltpu.VMEM((edges, width), F32),
@@ -234,7 +236,8 @@
         v_out,
         code.reshape(edges // tile, 1, tile),
         recv.reshape(edges // tile, 1, tile),
-        ext,
+        near,
+        far,
     )
 
 
@@ -244,16 +247,142 @@
     return bits
 
 
+class Swap:
+    def __init__(self, sign, near_src, far_src, near_dst, far_dst, sems):
+        self.row = lax.axis_index("row")
+        self.col = lax.axis_index("col")
+        self.rows = lax.axis_size("row")
+        self.cols = lax.axis_size("col")
+        self.peers = self.rows * self.cols
+        self.me = self.row * self.cols + self.col
+        self.sign = sign
+        self.near = (near_src, near_dst)
+        self.far = (far_src, far_dst)
+        self.near_send, self.near_recv, self.far_send, self.far_recv, self.own = sems
+
+    def place(self, peer):
+        return (peer // self.cols, peer % self.cols)
+
+    def greet(self):
+        barrier = pltpu.get_barrier_semaphore()
+
+        def signal(k, carry):
+            peer = self.place((self.me + k) % self.peers)
+            pl.semaphore_signal(barrier, inc=1, device_id=peer, device_id_type=MESH)
+            return carry
+
+        lax.fori_loop(1, self.peers, signal, 0)
+        pl.semaphore_wait(barrier, self.peers - 1)
+
+    def near_copy(self, k):
+        by = self.sign * (1, -1, 1, -1)[k]
+        row, col = self.row, self.col
+        if k < 2:
+            row = (row + by + self.rows) % self.rows
+        else:
+            col = (col + by + self.cols) % self.cols
+        return pltpu.make_async_remote_copy(
+            src_ref=self.near[0].at[k],
+            dst_ref=self.near[1].at[k],
+            send_sem=self.near_send.at[k],
+            recv_sem=self.near_recv.at[k],
+            device_id=(row, col),
+            device_id_type=MESH,
+        )
+
+    def far_copy(self, k):
+        peer = (self.me + k) % self.peers
+        return pltpu.make_async_remote_copy(
+            src_ref=self.far[0].at[peer],
+            dst_ref=self.far[1].at[self.me],
+            send_sem=self.far_send.at[k],
+            recv_sem=self.far_recv.at[k],
+            device_id=self.place(peer),
+            device_id_type=MESH,
+        )
+
+    def own_copy(self):
+        return pltpu.make_async_copy(
+            self.far[0].at[self.me], self.far[1].at[self.me], self.own.at[0]
+        )
+
+    def start(self):
+        for k in range(4):
+            self.near_copy(k).start()
+
+        def begin(k, carry):
+            self.far_copy(k).start()
+            return carry
+
+        lax.fori_loop(1, self.peers, begin, 0)
+        self.own_copy().start()
+
+    def wait(self):
+        for k in range(4):
+            self.near_copy(k).wait()
+
+        def end(k, carry):
+            self.far_copy(k).wait()
+            return carry
+
+        lax.fori_loop(1, self.peers, end, 0)
+        self.own_copy().wait()
+
+
+def swap_sems(peers):
+    dma = pltpu.SemaphoreType.DMA
+    return [dma((4,)), dma((4,)), dma((peers,)), dma((peers,)), dma((1,))]
+
+
+def halo_kernel(owner_ref, node_ref, near_ref, far_ref, near_s, far_s, *sems):
+    nodes = node_ref.shape[0]
+    near_rows = near_s.shape[0] * near_s.shape[1]
+    swap = Swap(1, near_s, far_s, near_ref, far_ref, sems)
+    offered = cross(col_hot(owner_ref[...], nodes), node_ref[...])
+    near_s[...] = offered[:near_rows].reshape(near_s.shape).astype(BF16)
+    far_s[...] = offered[near_rows:].reshape(far_s.shape).astype(BF16)
+    swap.greet()
+    swap.start()
+    swap.wait()
+
+
+def halo(owner, node, near_shape, far_shape):
+    vmem = pl.BlockSpec(memory_space=pltpu.VMEM)
+    return pl.pallas_call(
+        halo_kernel,
+        name="halo",
+        out_shape=(
+            jax.ShapeDtypeStruct(near_shape, BF16),
+            jax.ShapeDtypeStruct(far_shape, BF16),
+        ),
+        in_specs=[vmem] * 2,
+        out_specs=[vmem] * 2,
+        scratch_shapes=[pltpu.VMEM(near_shape, BF16), pltpu.VMEM(far_shape, BF16)]
+        + swap_sems(far_shape[0]),
+        compiler_params=pltpu.CompilerParams(collective_id=1, has_side_effects=True),
+        cost_estimate=pl.CostEstimate(flops=10**8, bytes_accessed=10**7, transcendentals=0),
+    )(owner, node)
+
+
 def scatter_kernel(orders, row_bits, col_bits, count, *refs):
     bits = row_bits + col_bits
-    inputs = refs[:count]
-    outputs = refs[count : 2 * count]
-    recv = [refs[2 * count + a * bits : 2 * count + (a + 1) * bits] for a in range(count)]
-    at = 2 * count + count * bits
-    held = [refs[at + a * (bits - 1) : at + (a + 1) * (bits - 1)] for a in range(count)]
-    send_sem, recv_sem = refs[-2:]
+    refs = list(refs)
+
+    def taken(number):
+        got = refs[:number]
+        del refs[:number]
+        return got
+
+    inputs = taken(count)
+    near_src, far_src = taken(2)
+    outputs = taken(count)
+    near_dst, far_dst = taken(2)
+    recv = [taken(bits) for _ in range(count)]
+    held = [taken(bits) for _ in range(count)]
+    send_sem, recv_sem, local_sem = taken(3)
     row = lax.axis_index("row")
     col = lax.axis_index("col")
+    swap = Swap(-1, near_src, far_src, near_dst, far_dst, refs)
 
     def mine(bit):
         if bit < row_bits:
@@ -267,11 +396,7 @@
         step = 1 << (bits - 1 - bit)
         return (row, col + step * (1 - 2 * mine(bit)))
 
-    barrier = pltpu.get_barrier_semaphore()
-    for bit in range(bits):
-        pl.semaphore_signal(barrier, inc=1, device_id=partner(bit), device_id_type=MESH)
-    pl.semaphore_wait(barrier, bits)
-
+    swap.greet()
     left = [list(range(bits)) for _ in range(count)]
     current = list(inputs)
 
@@ -291,6 +416,14 @@
     copies = [copy_of(a, 0) for a in range(count)]
     for item in copies:
         item.start()
+    swap.start()
+    kept = []
+    for a in range(count):
+        bit = orders[a][0]
+        place = left[a].index(bit)
+        spot = (slice(None),) * place + (mine(bit),)
+        kept.append(pltpu.make_async_copy(inputs[a].at[spot], held[a][0], local_sem.at[a]))
+        kept[a].start()
     sent = []
     for phase in range(bits):
         for a in range(count):
@@ -299,20 +432,26 @@
             bit = orders[a][phase]
             place = left[a].index(bit)
             spot = (slice(None),) * place + (mine(bit),)
-            value = current[a][spot].astype(F32) + recv[a][phase][...].astype(F32)
             left[a].remove(bit)
+            if phase == 0:
+                kept[a].wait()
+                own = held[a][0][...]
+            else:
+                own = current[a][spot]
+            value = own.astype(F32) + recv[a][phase][...].astype(F32)
             if phase == bits - 1:
                 outputs[a][...] = value
             else:
-                held[a][phase][...] = value.astype(BF16)
                 current[a] = held[a][phase]
+                current[a][...] = value.astype(BF16)
                 copies[a] = copy_of(a, phase + 1)
                 copies[a].start()
     for item in sent:
         item.wait_send()
-
-
-def scatter_sum(grads):
+    swap.wait()
+
+
+def scatter_sum(grads, near_grad, far_grad):
     rows_grid = lax.axis_size("row")
     cols_grid = lax.axis_size("col")
     row_bits = bit_count(rows_grid)
@@ -334,30 +473,55 @@
     ]
     count = len(grads)
     vmem = pl.BlockSpec(memory_space=pltpu.VMEM)
+    anywhere = pl.BlockSpec(memory_space=pl.ANY)
     recv = [
         pltpu.VMEM((2,) * (bits - 1 - phase) + (s, width), BF16)
         for s in slabs
         for phase in range(bits)
     ]
-    held = [
-        pltpu.VMEM((2,) * (bits - 1 - phase) + (s, width), BF16)
-        for s in slabs
-        for phase in range(bits - 1)
-    ]
+    shape = jax.ShapeDtypeStruct
+    dma = pltpu.SemaphoreType.DMA
     return pl.pallas_call(
         functools.partial(scatter_kernel, turns, row_bits, col_bits, count),
         name="scatter_sum",
-        out_shape=tuple(jax.ShapeDtypeStruct((s, width), F32) for s in slabs),
-        in_specs=[vmem] * count,
-        out_specs=[vmem] * count,
+        out_shape=tuple(shape((s, width), F32) for s in slabs)
+        + (shape(near_grad.shape, BF16), shape(far_grad.shape, BF16)),
+        in_specs=[anywhere] * count + [vmem] * 2,
+        out_specs=[vmem] * (count + 2),
         scratch_shapes=recv
-        + held
-        + [pltpu.SemaphoreType.DMA((count, bits)), pltpu.SemaphoreType.DMA((count, bits))],
+        + recv
+        + [dma((count, bits)), dma((count, bits)), dma((count,))]
+        + swap_sems(peers),
         compiler_params=pltpu.CompilerParams(
             collective_id=0, has_side_effects=True, vmem_limit_bytes=40 * 1024 * 1024
         ),
         cost_estimate=pl.CostEstimate(flops=10**9, bytes_accessed=10**8, transcendentals=0),
-    )(*shaped)
+    )(*shaped, near_grad, far_grad)
+
+
+def finish_kernel(count, owner_ref, part_ref, near_ref, far_ref, *refs):
+    nodes = part_ref.shape[0]
+    near = near_ref.shape[0]
+    sums = refs[:count]
+    grad_ref = refs[count]
+    hot = col_hot(owner_ref[...], nodes)
+    total = part_ref[...] + dot(hot[:, :near], near_ref[...])
+    grad_ref[...] = (total + dot(hot[:, near:], far_ref[...])).astype(BF16)
+    for source, target in zip(sums, refs[count + 1 :]):
+        target[...] = source[...]
+
+
+def finish(owner, part, near, far, sums):
+    vmem = pl.BlockSpec(memory_space=pltpu.VMEM)
+    count = len(sums)
+    return pl.pallas_call(
+        functools.partial(finish_kernel, count),
+        name="finish",
+        out_shape=(jax.ShapeDtypeStruct(part.shape, BF16),)
+        + tuple(jax.ShapeDtypeStruct(item.shape, F32) for item in sums),
+        in_specs=[vmem] * (4 + count),
+        out_specs=[vmem] * (1 + count),
+    )(owner, part, near, far, *sums)
 
 
 def shards(
@@ -377,23 +541,12 @@
     node_rows, width = node_latent.shape
     edge_rows = edge_latent.shape[0]
     peers = lax.axis_size("row") * lax.axis_size("col")
-    near_width = near_list.shape[2]
-    far_width = far_list.shape[2]
-    near_rows = 4 * near_width
-    moves = (("row", 1), ("row", -1), ("col", 1), ("col", -1))
-    owner = jnp.concatenate([near_list.reshape(-1), far_list.reshape(-1)], 0)
-    node_ids = jnp.arange(node_rows, dtype=jnp.int32)
-    offered = dot((owner[:, None] == node_ids[None, :]).astype(BF16), node_latent).astype(BF16)
-    parts = []
-    for slot, (axis, by) in enumerate(moves):
-        parts.append(
-            passed_along(offered[slot * near_width : (slot + 1) * near_width], axis, by)
-        )
-    far_send = offered[near_rows:].reshape(peers, far_width, width)
-    far_recv = lax.all_to_all(far_send, ("row", "col"), split_axis=0, concat_axis=0, tiled=True)
-    ext = jnp.concatenate(parts + [far_recv.reshape(peers * far_width, width)], 0)
+    near_shape = (4, near_list.shape[2], width)
+    far_shape = (peers, far_list.shape[2], width)
+    owner = jnp.concatenate([near_list.reshape(-1), far_list.reshape(-1)], 0)[None, :]
+    near, far = halo(owner, node_latent, near_shape, far_shape)
     scales = (1.0 / math.sqrt(edge_rows * peers), 1.0 / math.sqrt(node_rows * peers))
-    node_new, edge_new, part, grad_edge, ext_grad, g_in, g_out, h_in, h_out = compute(
+    node_new, edge_new, part, grad_edge, near_grad, far_grad, g_in, g_out, h_in, h_out = compute(
         node_latent,
         edge_latent,
         node_cotangent,
@@ -404,25 +557,16 @@
         w_node_out,
         sender_code,
         receiver,
-        ext,
+        near.reshape(-1, width),
+        far.reshape(-1, width),
         scales,
     )
-    back = []
-    for slot, (axis, by) in enumerate(moves):
-        back.append(
-            passed_along(ext_grad[slot * near_width : (slot + 1) * near_width], axis, -by)
-        )
-    far_back = lax.all_to_all(
-        ext_grad[near_rows:].reshape(peers, far_width, width),
-        ("row", "col"),
-        split_axis=0,
-        concat_axis=0,
-        tiled=True,
+    *sums, near_back, far_back = scatter_sum(
+        (g_in, h_in, g_out, h_out), near_grad.reshape(near_shape), far_grad.reshape(far_shape)
     )
-    returned = jnp.concatenate(back + [far_back.reshape(peers * far_width, width)], 0)
-    owner_hot = (node_ids[:, None] == owner[None, :]).astype(BF16)
-    grad_node = (part + dot(owner_hot, returned)).astype(BF16)
-    s_in, s_hin, s_out, s_hout = scatter_sum((g_in, h_in, g_out, h_out))
+    grad_node, s_in, s_hin, s_out, s_hout = finish(
+        owner, part, near_back.reshape(-1, width), far_back.reshape(-1, width), sums
+    )
     return (node_new, edge_new, grad_node, grad_edge, s_in, s_out, s_hin, s_hout)
 
 

time: 107 us -> 95.3 us (0.89)
  Pallas kernels: 54.9 us -> 81.5 us
  starting transfers between devices: 24.6 us -> 0 us
  waiting for transfers between devices: 10.5 us -> 0 us
  matrix products: 1.61 us -> 0 us
    pallas_call x0 -> x2, Pallas kernels: none -> 19.3 us  [the longest x1 17 us: halo(): pl.pallas_call(halo_kernel, name='halo', out_shape=(jax.ShapeDtypeStruct(...]
    ppermute x8 -> x0, starting transfers between devices: 16.4 us -> none  [passed_along(): lax.ppermute(value, axis, [(i, (i + by) % peers) for i in range(peers)])]
    all_to_all x2 -> x0, starting transfers between devices: 8.17 us -> none  [the longest x1 4.89 us: shards(): lax.all_to_all(far_send, ('row', 'col'), split_axis=0, concat_axis=0, til...]
    ppermute x8 -> x0, waiting for transfers between devices: 7.97 us -> none  [passed_along(): lax.ppermute(value, axis, [(i, (i + by) % peers) for i in range(peers)])]
    pallas_call x1, Pallas kernels: 28.7 us -> 35.6 us  [scatter_sum(): pl.pallas_call(functools.partial(scatter_kernel, turns, row_bits, col_bit...]
    all_to_all x2 -> x0, waiting for transfers between devices: 2.53 us -> none  [the longest x1 2.53 us: shards(): lax.all_to_all(far_send, ('row', 'col'), split_axis=0, concat_axis=0, til...]
    unnamed x26 -> x25, local copies, waits for them, and re-layouts: 8.83 us -> 11.2 us
    reshape x4 -> x2, local copies, waits for them, and re-layouts: 3.24 us -> 0.85 us  [the longest x1 0.76 us: shards(): near_list.reshape(-1)]
  transfers between devices with their start and end apart: 10 -> 0, of which waited for: 3 -> 0; matrix products, arithmetic and copies ran while one was open for 1% -> 0% of each run, Pallas kernels for 27% -> 0%
where the time goes in v2:
time: 95.3 us; the launch traced here: 94.9 us
  Pallas kernels  81.5 us (86%)
  local copies, waits for them, and re-layouts  12.1 us (13%)
    pallas_call x1, Pallas kernels, scatter_sum(): pl.pallas_call(functools.partial(scatter_kernel, turns, row_bits, col_bit...  35.6 us
    pallas_call x1, Pallas kernels, compute(): pl.pallas_call(functools.partial(compute_kernel, tile, *scales), name='pr...  26.6 us
    pallas_call x1, Pallas kernels, halo(): pl.pallas_call(halo_kernel, name='halo', out_shape=(jax.ShapeDtypeStruct(...  17 us
    unnamed x25, local copies, waits for them, and re-layouts  11.2 us
    pallas_call x1, Pallas kernels, finish(): pl.pallas_call(functools.partial(finish_kernel, count), name='finish', ou...  2.25 us

profile of v2, /device:TPU:0, one launch (start us, length us, event | category | flops | bytes accessed | tf_op | source)
XLA Modules:
  0.0 94.9 jit_solution(10955916386329778320)
XLA Ops:
  0.6 0.8 reshape.60
  1.4 0.8 copy.20
  2.2 0.1 reshape.61
  2.2 0.6 pad_add_fusion
  2.8 17.0 %halo.1 = (bf16[4,64,512]{2,1,0:T(8,128)(2,1)}, bf16[32,8,512]{2,1,0:T(8,128)(2,1)}) custom-call(s32[1,512]{1,0:T(1,128)} %bitcast.21, bf16[256,512]{1,0:T(8,128)(2,1)} %node_ref.3), custom_call_target="tpu_custom_call" | custom-call | flops 100000000 | bytes 10000000 | tf_op jit(solution)/shard_map/halo/pallas_call | solution.py:351
  19.9 26.6 %processor.1 = (bf16[256,512]{1,0:T(8,128)(2,1)}, bf16[2048,512]{1,0:T(8,128)(2,1)}, f32[256,512]{1,0:T(8,128)}, bf16[2048,512]{1,0:T(8,128)(2,1)}, bf16[256,512...) custom-call(bf16[256,512]{1,0:T(8,128)(2,1)} %node_ref.3, ...), custom_call_target="tpu_custom_call" | custom-call | flops 10737418240 | bytes 41943040 | tf_op jit(solution)/shard_map/processor/pallas_call | solution.py:197
  46.5 0.0 copy-start
  46.5 1.4 %copy-done = bf16[1536,512]{1,0:T(8,128)(2,1)S(1)} copy-done((bf16[1536,512]{1,0:T(8,128)(2,1)S(1)}, bf16[1536,512]{1,0:T(8,128)(2,1)}, u32[]{:S(2)}) %copy-start) | copy-done | bytes 1572888
  47.9 0.0 copy-start.1
  47.9 1.2 %copy-done.1 = bf16[1024,512]{1,0:T(8,128)(2,1)S(1)} copy-done((bf16[1024,512]{1,0:T(8,128)(2,1)S(1)}, bf16[1024,512]{1,0:T(8,128)(2,1)}, u32[]{:S(2)}) %copy-start.1) | copy-done | bytes 1048600
  49.1 0.0 copy-start.2
  49.1 1.0 %copy-done.2 = bf16[512,512]{1,0:T(8,128)(2,1)S(1)} copy-done((bf16[512,512]{1,0:T(8,128)(2,1)S(1)}, bf16[512,512]{1,0:T(8,128)(2,1)}, u32[]{:S(2)}) %copy-start.2) | copy-done | bytes 524312
  50.2 1.0 %copy-done.3 = bf16[512,512]{1,0:T(8,128)(2,1)S(1)} copy-done((bf16[512,512]{1,0:T(8,128)(2,1)S(1)}, bf16[512,512]{1,0:T(8,128)(2,1)}, u32[]{:S(2)}) %copy-start.3) | copy-done | bytes 524312
  51.2 0.9 copy-done.6
  52.2 0.9 copy-done.7
  53.1 35.6 %scatter_sum.1 = (f32[48,512]{1,0:T(8,128)S(1)}, f32[32,512]{1,0:T(8,128)S(1)}, f32[16,512]{1,0:T(8,128)S(1)}, f32[16,512]{1,0:T(8,128)S(1)}, bf16[4,64,512]{2,1...) custom-call(bf16[2,2,2,2,2,48,512]{6,5,4,3,2,1,0:T(8,128)(2,1)S(1)} %bitcast.13, ...), custom_call_target="tpu_custom_call" | custom-call | flops 1000000000 | bytes 100000000 | tf_op jit(solution)/shard_map/scatter_sum/pallas_call | solution.py:484
  88.7 0.0 copy-start.4
  88.8 0.7 copy-done.4
  89.4 0.7 copy-done.5
  90.1 0.6 copy-done.8
  90.8 0.6 copy-done.9
  91.4 0.6 copy-done.10
  92.0 0.6 copy-done.11
  92.6 2.2 %finish.1 = (bf16[256,512]{1,0:T(8,128)(2,1)}, f32[48,512]{1,0:T(8,128)}, f32[32,512]{1,0:T(8,128)}, f32[16,512]{1,0:T(8,128)}, f32[16,512]{1,0:T(8,128)}) custom-call(s32[1,512]{1,0:T(1,128)} %bitcast.22, f32[256,512]{1,0:T(8,128)} %get-tuple-element.35.part_ref, bf16[256,512]{1,0:T(8,128)(2,1)} %bitcast.17, bf16[256,512]{1,0:T(8,128)(2,1)} %bitcast.18, ...), custom_call_target="tpu_custom_call" | custom-call | tf_op jit(solution)/shard_map/finish/pallas_call | solution.py:517
  (8 shorter events, 0.0 us)
Async XLA Ops:
  46.5 1.4 %copy-start = (bf16[1536,512]{1,0:T(8,128)(2,1)S(1)}, bf16[1536,512]{1,0:T(8,128)(2,1)}, u32[]{:S(2)}) copy-start(bf16[1536,512]{1,0:T(8,128)(2,1)} %get-tuple-element.36) | copy-start | bytes 4718596
  47.9 1.2 %copy-start.1 = (bf16[1024,512]{1,0:T(8,128)(2,1)S(1)}, bf16[1024,512]{1,0:T(8,128)(2,1)}, u32[]{:S(2)}) copy-start(bf16[1024,512]{1,0:T(8,128)(2,1)} %get-tuple-element.37) | copy-start | bytes 3145732
  49.1 1.0 %copy-start.2 = (bf16[512,512]{1,0:T(8,128)(2,1)S(1)}, bf16[512,512]{1,0:T(8,128)(2,1)}, u32[]{:S(2)}) copy-start(bf16[512,512]{1,0:T(8,128)(2,1)} %get-tuple-element.38) | copy-start | bytes 1572868
  50.2 1.0 %copy-start.3 = (bf16[512,512]{1,0:T(8,128)(2,1)S(1)}, bf16[512,512]{1,0:T(8,128)(2,1)}, u32[]{:S(2)}) copy-start(bf16[512,512]{1,0:T(8,128)(2,1)} %get-tuple-element.39) | copy-start | bytes 1572868
  51.2 0.9 %copy-start.6 = (bf16[256,512]{1,0:T(8,128)(2,1)S(1)}, bf16[256,512]{1,0:T(8,128)(2,1)}, u32[]{:S(2)}) copy-start(bf16[256,512]{1,0:T(8,128)(2,1)} %get-tuple-element.40) | copy-start | bytes 786436
  52.2 0.9 %copy-start.7 = (bf16[256,512]{1,0:T(8,128)(2,1)S(1)}, bf16[256,512]{1,0:T(8,128)(2,1)}, u32[]{:S(2)}) copy-start(bf16[256,512]{1,0:T(8,128)(2,1)} %get-tuple-element.41) | copy-start | bytes 786436
  88.7 0.7 copy-start.4
  89.4 0.7 copy-start.5
  90.1 0.6 copy-start.8
  90.8 0.6 copy-start.9
  91.4 0.6 copy-start.10
  92.0 0.6 copy-start.11

commit v3 on v2

--- a/solution.py
+++ b/solution.py
@@ -524,6 +524,395 @@
     )(owner, part, near, far, *sums)
 
 
+class Halving:
+    def __init__(self, order, row_bits, col_bits, source, recv, held, out, send_sem, recv_sem):
+        self.order = order
+        self.row_bits = row_bits
+        self.bits = row_bits + col_bits
+        self.left = list(range(self.bits))
+        self.current = source
+        self.recv, self.held, self.out = recv, held, out
+        self.send_sem, self.recv_sem = send_sem, recv_sem
+        self.sent = []
+        self.phase = 0
+
+    def mine(self, bit):
+        if bit < self.row_bits:
+            return (lax.axis_index("row") // (1 << (self.row_bits - 1 - bit))) % 2
+        return (lax.axis_index("col") // (1 << (self.bits - 1 - bit))) % 2
+
+    def partner(self, bit):
+        row, col = lax.axis_index("row"), lax.axis_index("col")
+        if bit < self.row_bits:
+            return (row + (1 << (self.row_bits - 1 - bit)) * (1 - 2 * self.mine(bit)), col)
+        return (row, col + (1 << (self.bits - 1 - bit)) * (1 - 2 * self.mine(bit)))
+
+    def spot(self, bit, which):
+        return (slice(None),) * self.left.index(bit) + (which,)
+
+    def start(self):
+        bit = self.order[self.phase]
+        copy = pltpu.make_async_remote_copy(
+            src_ref=self.current.at[self.spot(bit, 1 - self.mine(bit))],
+            dst_ref=self.recv[self.phase],
+            send_sem=self.send_sem.at[self.phase],
+            recv_sem=self.recv_sem.at[self.phase],
+            device_id=self.partner(bit),
+            device_id_type=MESH,
+        )
+        copy.start()
+        self.sent.append(copy)
+
+    def step(self):
+        bit = self.order[self.phase]
+        self.sent[-1].wait_recv()
+        own = self.current[self.spot(bit, self.mine(bit))]
+        value = own.astype(F32) + self.recv[self.phase][...].astype(F32)
+        self.left.remove(bit)
+        self.phase += 1
+        if self.phase == self.bits:
+            self.out[...] = value
+            return
+        self.current = self.held[self.phase - 1]
+        self.current[...] = value.astype(BF16)
+        self.start()
+
+    def end(self):
+        for copy in self.sent:
+            copy.wait_send()
+
+
+def whole_kernel(tile, scales, turns, row_bits, col_bits, *refs):
+    edge_scale, node_scale = scales
+    bits = row_bits + col_bits
+    refs = list(refs)
+
+    def taken(number):
+        got = refs[:number]
+        del refs[:number]
+        return got
+
+    owner_ref, node_ref, ncot_ref, code_ref, recv_ref = taken(5)
+    loads = taken(6)
+    node_new_ref, edge_new_ref, grad_edge_ref, part_ref, near_back, far_back = taken(6)
+    outputs = taken(4)
+    proj, slope, normed_s, recip_s, hidden_s, gath_s, gg_s, sums_s, acc_e, acc_o = taken(10)
+    held_in = taken(6)
+    edge_new_s, grad_edge_s = taken(2)
+    near_s, far_s, near_r, far_r, near_g, far_g = taken(6)
+    grads = taken(4)
+    recv = [taken(bits) for _ in range(4)]
+    held = [taken(bits - 1) for _ in range(4)]
+    send_sem, recv_sem, load_sem, store_sem = taken(4)
+    out_swap = Swap(1, near_s, far_s, near_r, far_r, taken(5))
+    back_swap = Swap(-1, near_g, far_g, near_back, far_back, taken(5))
+
+    copies = []
+    for k in (0, 2, 3, 4, 5, 1):
+        copies.append(pltpu.make_async_copy(loads[k], held_in[k], load_sem.at[k]))
+        copies[-1].start()
+    edge_s, ecot_s, w_in, w_out, v_in, v_out = held_in
+    edge_copy, w_in_copy, w_out_copy, v_in_copy, v_out_copy, ecot_copy = copies
+
+    nodes, width = node_ref.shape
+    edges = edge_s.shape[0]
+    near = near_s.shape[0] * near_s.shape[1]
+    far = far_s.shape[0] * far_s.shape[1]
+    rows = nodes + near + far
+    steps = edges // tile
+    w_e = w_in.at[pl.ds(0, width)]
+    w_s = w_in.at[pl.ds(width, width)]
+    w_r = w_in.at[pl.ds(2 * width, width)]
+    v_a = v_in.at[pl.ds(0, width)]
+    v_b = v_in.at[pl.ds(width, width)]
+
+    def span_of(step):
+        return pl.ds(pl.multiple_of(step * tile, tile), tile)
+
+    offered = cross(col_hot(owner_ref[...], nodes), node_ref[...])
+    near_s[...] = offered[:near].reshape(near_s.shape).astype(BF16)
+    far_s[...] = offered[near:].reshape(far_s.shape).astype(BF16)
+    out_swap.greet()
+    out_swap.start()
+
+    edge_copy.wait()
+    w_in_copy.wait()
+    gath_s[...] = jnp.zeros_like(gath_s)
+    sums_s[...] = jnp.zeros_like(sums_s)
+    acc_e[...] = jnp.zeros_like(acc_e)
+    acc_o[...] = jnp.zeros_like(acc_o)
+    proj[pl.ds(0, nodes), :] = dot(node_ref[...], w_s[...]).astype(BF16)
+    proj[pl.ds(rows, nodes), :] = dot(node_ref[...], w_r[...]).astype(BF16)
+
+    def ahead(step, carry):
+        span = span_of(step)
+        hot = row_hot(recv_ref[step], nodes)
+        slope[span, :] = dot(edge_s[span, :], w_e[...]) + dot(hot, proj[pl.ds(rows, nodes), :])
+        return carry
+
+    lax.fori_loop(0, steps, ahead, 0)
+    w_out_copy.wait()
+    v_in_copy.wait()
+    v_out_copy.wait()
+    ecot_copy.wait()
+    out_swap.wait()
+    near_rows = near_r[...].astype(F32).reshape(near, width).astype(BF16)
+    far_rows = far_r[...].astype(F32).reshape(far, width).astype(BF16)
+    proj[pl.ds(nodes, near), :] = dot(near_rows, w_s[...]).astype(BF16)
+    proj[pl.ds(nodes + near, far), :] = dot(far_rows, w_s[...]).astype(BF16)
+
+    def forward(step, carry):
+        span = span_of(step)
+        edge = edge_s[span, :]
+        pre = slope[span, :] + dot(row_hot(code_ref[step], rows), proj[pl.ds(0, rows), :])
+        sigma = jax.nn.sigmoid(pre)
+        slope[span, :] = sigma * (1.0 + pre * (1.0 - sigma))
+        hidden = (pre * sigma).astype(BF16)
+        hidden_s[span, :] = hidden
+        normed, recip = norm_parts(dot(hidden, w_out[...]))
+        normed_s[span, :] = normed
+        recip_s[span, :] = jnp.broadcast_to(recip, (tile, 128))
+        new = (edge.astype(F32) + normed).astype(BF16)
+        edge_new_s[span, :] = new
+        gath_s[...] += dot(col_hot(recv_ref[step], nodes), new)
+        return carry
+
+    lax.fori_loop(0, steps, forward, 0)
+    edge_new_copy = pltpu.make_async_copy(edge_new_s, edge_new_ref, store_sem.at[0])
+    edge_new_copy.start()
+
+    node = node_ref[...]
+    gathered = gath_s[...].astype(BF16)
+    pre = dot(node, v_a[...]) + dot(gathered, v_b[...])
+    sigma = jax.nn.sigmoid(pre)
+    hidden = (pre * sigma).astype(BF16)
+    normed, recip = norm_parts(dot(hidden, v_out[...]))
+    node_new_ref[...] = (node.astype(F32) + normed).astype(BF16)
+    ncot = ncot_ref[...].astype(F32)
+    delta = norm_back(normed, recip, ncot).astype(BF16)
+    pre_delta = (dot_t(delta, v_out[...]) * (sigma * (1.0 + pre * (1.0 - sigma)))).astype(BF16)
+    g_in, h_in, g_out, h_out = grads
+    h_in[pl.ds(0, width), :] = (cross(node, pre_delta) * node_scale).astype(BF16)
+    h_in[pl.ds(width, width), :] = (cross(gathered, pre_delta) * node_scale).astype(BF16)
+    h_out[...] = (cross(hidden, delta) * node_scale).astype(BF16)
+
+    halvings = []
+    for a in range(4):
+        slab, _ = outputs[a].shape
+        source = grads[a].reshape((2,) * bits + (slab, width))
+        halvings.append(
+            Halving(
+                turns[a],
+                row_bits,
+                col_bits,
+                source,
+                recv[a],
+                held[a],
+                outputs[a],
+                send_sem.at[a],
+                recv_sem.at[a],
+            )
+        )
+    from_edges = (halvings[0], halvings[2])
+    from_nodes = (halvings[1], halvings[3])
+    for item in from_nodes:
+        item.start()
+    gg_s[...] = dot_t(pre_delta, v_b[...]).astype(BF16)
+    part_ref[...] = ncot + dot_t(pre_delta, v_a[...])
+
+    def backward(step, carry):
+        span = span_of(step)
+        recvs = recv_ref[step]
+        total = ecot_s[span, :].astype(F32) + dot(row_hot(recvs, nodes), gg_s[...])
+        recip = recip_s[span, :][:, :1]
+        delta = norm_back(normed_s[span, :], recip, total).astype(BF16)
+        normed_s[span, :] = total
+        pre_delta = (dot_t(delta, w_out[...]) * slope[span, :]).astype(BF16)
+        acc_o[...] += cross(hidden_s[span, :], delta)
+        hidden_s[span, :] = pre_delta
+        sums_s[pl.ds(0, rows), :] += dot(col_hot(code_ref[step], rows), pre_delta)
+        sums_s[pl.ds(rows, nodes), :] += dot(col_hot(recvs, nodes), pre_delta)
+        acc_e[...] += cross(edge_s[span, :], pre_delta)
+        return carry
+
+    half = steps // 2
+    lax.fori_loop(0, half, backward, 0)
+    for item in from_nodes:
+        item.step()
+    lax.fori_loop(half, steps, backward, 0)
+    for item in from_nodes:
+        item.step()
+
+    g_in[pl.ds(0, width), :] = (acc_e[...] * edge_scale).astype(BF16)
+    g_out[...] = (acc_o[...] * edge_scale).astype(BF16)
+    own_sum = sums_s[pl.ds(0, nodes), :].astype(BF16)
+    near_sum = sums_s[pl.ds(nodes, near), :].astype(BF16)
+    far_sum = sums_s[pl.ds(nodes + near, far), :].astype(BF16)
+    recv_sum = sums_s[pl.ds(rows, nodes), :].astype(BF16)
+    sent = cross(node, own_sum) + cross(near_rows, near_sum) + cross(far_rows, far_sum)
+    g_in[pl.ds(width, width), :] = (sent * edge_scale).astype(BF16)
+    g_in[pl.ds(2 * width, width), :] = (cross(node, recv_sum) * edge_scale).astype(BF16)
+    for item in from_edges:
+        item.start()
+    near_g[...] = dot_t(near_sum, w_s[...]).reshape(near_g.shape).astype(BF16)
+    far_g[...] = dot_t(far_sum, w_s[...]).reshape(far_g.shape).astype(BF16)
+    back_swap.start()
+    part_ref[...] += dot_t(own_sum, w_s[...]) + dot_t(recv_sum, w_r[...])
+
+    def behind(step, carry):
+        span = span_of(step)
+        change = dot_t(hidden_s[span, :], w_e[...])
+        grad_edge_s[span, :] = (normed_s[span, :] + change).astype(BF16)
+        return carry
+
+    lax.fori_loop(0, steps, behind, 0)
+    grad_edge_copy = pltpu.make_async_copy(grad_edge_s, grad_edge_ref, store_sem.at[1])
+    grad_edge_copy.start()
+    for phase in range(bits):
+        for item in halvings:
+            if item.phase <= phase:
+                item.step()
+    for item in halvings:
+        item.end()
+    back_swap.wait()
+    edge_new_copy.wait()
+    grad_edge_copy.wait()
+
+
+def whole(owner, node, ncot, code, recv_at, big, near_shape, far_shape, scales):
+    row_bits = bit_count(lax.axis_size("row"))
+    col_bits = bit_count(lax.axis_size("col"))
+    bits = row_bits + col_bits
+    peers = 1 << bits
+    nodes, width = node.shape
+    edges = big[0].shape[0]
+    rows = nodes + near_shape[0] * near_shape[1] + far_shape[0] * far_shape[1]
+    tile = math.gcd(edges, 512)
+    grad_shapes = [big[2].shape, big[4].shape, big[3].shape, big[5].shape]
+    slabs = [item[0] // peers for item in grad_shapes]
+    core = bits - 1
+    along_col = list(range(bits - 2, row_bits - 1, -1))
+    row_near = [row_bits - 1]
+    row_far = list(range(row_bits - 2, -1, -1))
+    turns = [
+        [core] + along_col + row_near + row_far,
+        [core] + row_near + row_far + along_col,
+        [core] + row_near + row_far + along_col,
+        [core] + row_far + along_col + row_near,
+    ]
+    vmem = pl.BlockSpec(memory_space=pltpu.VMEM)
+    anywhere = pl.BlockSpec(memory_space=pl.ANY)
+    shape = jax.ShapeDtypeStruct
+    dma = pltpu.SemaphoreType.DMA
+    scratch = pltpu.VMEM
+    return pl.pallas_call(
+        functools.partial(whole_kernel, tile, scales, turns, row_bits, col_bits),
+        name="whole_step",
+        out_shape=(
+            shape((nodes, width), BF16),
+            shape((edges, width), BF16),
+            shape((edges, width), BF16),
+            shape((nodes, width), F32),
+            shape(near_shape, BF16),
+            shape(far_shape, BF16),
+        )
+        + tuple(shape((s, width), F32) for s in slabs),
+        in_specs=[vmem] * 5 + [anywhere] * 6,
+        out_specs=[vmem, anywhere, anywhere] + [vmem] * 7,
+        scratch_shapes=[
+            scratch((rows + nodes, width), BF16),
+            scratch((edges, width), F32),
+            scratch((edges, width), F32),
+            scratch((edges, 128), F32),
+            scratch((edges, width), BF16),
+            scratch((nodes, width), F32),
+            scratch((nodes, width), BF16),
+            scratch((rows + nodes, width), F32),
+            scratch((width, width), F32),
+            scratch((width, width), F32),
+        ]
+        + [scratch(item.shape, BF16) for item in big]
+        + [scratch((edges, width), BF16)] * 2
+        + [scratch(near_shape, BF16), scratch(far_shape, BF16)] * 3
+        + [scratch(item, BF16) for item in grad_shapes]
+        + [
+            scratch((2,) * (bits - 1 - phase) + (s, width), BF16)
+            for s in slabs
+            for phase in range(bits)
+        ]
+        + [
+            scratch((2,) * (bits - 1 - phase) + (s, width), BF16)
+            for s in slabs
+            for phase in range(bits - 1)
+        ]
+        + [dma((4, bits)), dma((4, bits)), dma((6,)), dma((2,))]
+        + swap_sems(peers)
+        + swap_sems(peers),
+        compiler_params=pltpu.CompilerParams(
+            collective_id=2, has_side_effects=True, vmem_limit_bytes=67043328
+        ),
+        cost_estimate=pl.CostEstimate(flops=10**10, bytes_accessed=10**8, transcendentals=0),
+    )(
+        owner,
+        node,
+        ncot,
+        code.reshape(edges // tile, 1, tile),
+        recv_at.reshape(edges // tile, 1, tile),
+        *big,
+    )
+
+
+def close_kernel(count, owner_ref, part_ref, near_ref, far_ref, *refs):
+    refs = list(refs)
+    sums = refs[:4]
+    passed = refs[4 : 4 + count]
+    grad_ref = refs[4 + count]
+    targets = refs[5 + count : 9 + count]
+    passed_out = refs[9 + count : 9 + 2 * count]
+    held = refs[9 + 2 * count : 9 + 3 * count]
+    sem = refs[-1]
+    into = [
+        pltpu.make_async_copy(a, b, sem.at[0, k]) for k, (a, b) in enumerate(zip(passed, held))
+    ]
+    out = [
+        pltpu.make_async_copy(a, b, sem.at[1, k])
+        for k, (a, b) in enumerate(zip(held, passed_out))
+    ]
+    for copy in into:
+        copy.start()
+    nodes = part_ref.shape[0]
+    near = near_ref.shape[0]
+    hot = col_hot(owner_ref[...], nodes)
+    total = part_ref[...] + dot(hot[:, :near], near_ref[...])
+    grad_ref[...] = (total + dot(hot[:, near:], far_ref[...])).astype(BF16)
+    for source, target in zip(sums, targets):
+        target[...] = source[...]
+    for one, two in zip(into, out):
+        one.wait()
+        two.start()
+    for copy in out:
+        copy.wait()
+
+
+def close(owner, part, near, far, sums, passed):
+    vmem = pl.BlockSpec(memory_space=pltpu.VMEM)
+    anywhere = pl.BlockSpec(memory_space=pl.ANY)
+    count = len(passed)
+    shape = jax.ShapeDtypeStruct
+    return pl.pallas_call(
+        functools.partial(close_kernel, count),
+        name="close",
+        out_shape=(shape(part.shape, BF16),)
+        + tuple(shape(item.shape, F32) for item in sums)
+        + tuple(shape(item.shape, BF16) for item in passed),
+        in_specs=[vmem] * 8 + [anywhere] * count,
+        out_specs=[vmem] * 5 + [anywhere] * count,
+        scratch_shapes=[pltpu.VMEM(item.shape, BF16) for item in passed]
+        + [pltpu.SemaphoreType.DMA((2, count))],
+        compiler_params=pltpu.CompilerParams(vmem_limit_bytes=67043328),
+    )(owner, part, near, far, *sums, *passed)
+
+
 def shards(
     node_latent,
     edge_latent,
@@ -544,8 +933,30 @@
     near_shape = (4, near_list.shape[2], width)
     far_shape = (peers, far_list.shape[2], width)
     owner = jnp.concatenate([near_list.reshape(-1), far_list.reshape(-1)], 0)[None, :]
+    scales = (1.0 / math.sqrt(edge_rows * peers), 1.0 / math.sqrt(node_rows * peers))
+    big = (edge_latent, edge_cotangent, w_edge_in, w_edge_out, w_node_in, w_node_out)
+    if all(item.shape[0] % (16 * peers) == 0 for item in big[2:]):
+        node_new, edge_new, grad_edge, part, near_back, far_back, *sums = whole(
+            owner,
+            node_latent,
+            node_cotangent,
+            sender_code,
+            receiver,
+            big,
+            near_shape,
+            far_shape,
+            scales,
+        )
+        grad_node, s_in, s_hin, s_out, s_hout, node_new, edge_new, grad_edge = close(
+            owner,
+            part,
+            near_back.reshape(-1, width),
+            far_back.reshape(-1, width),
+            sums,
+            (node_new, edge_new, grad_edge),
+        )
+        return (node_new, edge_new, grad_node, grad_edge, s_in, s_out, s_hin, s_hout)
     near, far = halo(owner, node_latent, near_shape, far_shape)
-    scales = (1.0 / math.sqrt(edge_rows * peers), 1.0 / math.sqrt(node_rows * peers))
     node_new, edge_new, part, grad_edge, near_grad, far_grad, g_in, g_out, h_in, h_out = compute(
         node_latent,
         edge_latent,

time: 95.3 us -> 80.1 us (0.84)
  local copies, waits for them, and re-layouts: 12.1 us -> 1.61 us
  Pallas kernels: 81.5 us -> 77 us
    unnamed x25 -> x1, local copies, waits for them, and re-layouts: 11.2 us -> 0.76 us
    pallas_call x4 -> x2, Pallas kernels: 81.5 us -> 77 us  [the longest x1 71.2 us: whole(): pl.pallas_call(functools.partial(whole_kernel, tile, scales, turns, row_b...]
where the time goes in v3:
time: 80.1 us; the launch traced here: 79.9 us
  Pallas kernels  77 us (96%)
  local copies, waits for them, and re-layouts  1.61 us (2%)
    pallas_call x1, Pallas kernels, whole(): pl.pallas_call(functools.partial(whole_kernel, tile, scales, turns, row_b...  71.2 us
    pallas_call x1, Pallas kernels, close(): pl.pallas_call(functools.partial(close_kernel, count), name='close', out_...  5.84 us

profile of v3, /device:TPU:0, one launch (start us, length us, event | category | flops | bytes accessed | tf_op | source)
XLA Modules:
  0.0 79.9 jit_solution(3558778579447068594)
XLA Ops:
  0.6 0.8 reshape.34
  1.4 0.8 copy.20
  2.2 0.1 reshape.35
  2.2 0.6 pad_add_fusion
  2.8 71.2 %whole_step.1 = (bf16[256,512]{1,0:T(8,128)(2,1)}, bf16[2048,512]{1,0:T(8,128)(2,1)}, bf16[2048,512]{1,0:T(8,128)(2,1)}, f32[256,512]{1,0:T(8,128)}, bf16[4,64,5...) custom-call(s32[1,512]{1,0:T(1,128)} %bitcast.7, ...), custom_call_target="tpu_custom_call" | custom-call | flops 10000000000 | bytes 100000000 | tf_op jit(solution)/shard_map/whole_step/pallas_call | solution.py:808
  74.0 5.8 %close.1 = (bf16[256,512]{1,0:T(8,128)(2,1)}, f32[48,512]{1,0:T(8,128)}, f32[32,512]{1,0:T(8,128)}, f32[16,512]{1,0:T(8,128)}, f32[16,512]{1,0:T(8,128)}, /*inde...) custom-call(s32[1,512]{1,0:T(1,128)} %bitcast.8, f32[256,512]{1,0:T(8,128)} %get-tuple-element.26.part_ref, ...), custom_call_target="tpu_custom_call" | custom-call | tf_op jit(solution)/shard_map/close/pallas_call | solution.py:902

commit v4 on v3

--- a/solution.py
+++ b/solution.py
@@ -56,6 +56,19 @@
     tile = codes.shape[1]
     ids = lax.broadcasted_iota(jnp.int32, (count, tile), 0)
     return jnp.where(codes == ids, 1.0, 0.0).astype(BF16)
+
+
+def flat(lists):
+    high, low = lists.shape
+    count = high * low
+    spread = lax.broadcasted_iota(jnp.int32, (low, count), 1) % low
+    spread = jnp.where(spread == lax.broadcasted_iota(jnp.int32, (low, count), 0), 1.0, 0.0)
+    wide = jnp.dot(
+        lists.astype(F32), spread, precision=lax.Precision.HIGHEST, preferred_element_type=F32
+    )
+    keep = lax.broadcasted_iota(jnp.int32, (high, count), 1) // low
+    keep = keep == lax.broadcasted_iota(jnp.int32, (high, count), 0)
+    return jnp.sum(jnp.where(keep, wide, 0.0), 0, keepdims=True).astype(jnp.int32)
 
 
 def compute_kernel(
@@ -525,7 +538,7 @@
 
 
 class Halving:
-    def __init__(self, order, row_bits, col_bits, source, recv, held, out, send_sem, recv_sem):
+    def __init__(self, order, row_bits, col_bits, source, recv, held, out, send_sem, recv_sem, at):
         self.order = order
         self.row_bits = row_bits
         self.bits = row_bits + col_bits
@@ -533,6 +546,7 @@
         self.current = source
         self.recv, self.held, self.out = recv, held, out
         self.send_sem, self.recv_sem = send_sem, recv_sem
+        self.at = at
         self.sent = []
         self.phase = 0
 
@@ -548,7 +562,11 @@
         return (row, col + (1 << (self.bits - 1 - bit)) * (1 - 2 * self.mine(bit)))
 
     def spot(self, bit, which):
-        return (slice(None),) * self.left.index(bit) + (which,)
+        lead = [slice(None)] * len(self.left)
+        lead[self.left.index(bit)] = which
+        if self.phase == 0 and self.at is not None:
+            lead.append(pl.ds(self.at, 16))
+        return tuple(lead)
 
     def start(self):
         bit = self.order[self.phase]
@@ -571,7 +589,10 @@
         self.left.remove(bit)
         self.phase += 1
         if self.phase == self.bits:
-            self.out[...] = value
+            if self.at is None:
+                self.out[...] = value
+            else:
+                self.out[pl.ds(self.at, 16), :] = value
             return
         self.current = self.held[self.phase - 1]
         self.current[...] = value.astype(BF16)
@@ -582,7 +603,7 @@
             copy.wait_send()
 
 
-def whole_kernel(tile, scales, turns, row_bits, col_bits, *refs):
+def whole_kernel(tile, scales, pieces, turns, row_bits, col_bits, *refs):
     edge_scale, node_scale = scales
     bits = row_bits + col_bits
     refs = list(refs)
@@ -592,7 +613,7 @@
         del refs[:number]
         return got
 
-    owner_ref, node_ref, ncot_ref, code_ref, recv_ref = taken(5)
+    near_list, far_list, node_ref, ncot_ref, code_ref, recv_ref = taken(6)
     loads = taken(6)
     node_new_ref, edge_new_ref, grad_edge_ref, part_ref, near_back, far_back = taken(6)
     outputs = taken(4)
@@ -601,8 +622,8 @@
     edge_new_s, grad_edge_s = taken(2)
     near_s, far_s, near_r, far_r, near_g, far_g = taken(6)
     grads = taken(4)
-    recv = [taken(bits) for _ in range(4)]
-    held = [taken(bits - 1) for _ in range(4)]
+    recv = [taken(bits) for _ in pieces]
+    held = [taken(bits - 1) for _ in pieces]
     send_sem, recv_sem, load_sem, store_sem = taken(4)
     out_swap = Swap(1, near_s, far_s, near_r, far_r, taken(5))
     back_swap = Swap(-1, near_g, far_g, near_back, far_back, taken(5))
@@ -627,11 +648,14 @@
     v_b = v_in.at[pl.ds(width, width)]
 
     def span_of(step):
+        if isinstance(step, int):
+            return pl.ds(step * tile, tile)
         return pl.ds(pl.multiple_of(step * tile, tile), tile)
 
-    offered = cross(col_hot(owner_ref[...], nodes), node_ref[...])
-    near_s[...] = offered[:near].reshape(near_s.shape).astype(BF16)
-    far_s[...] = offered[near:].reshape(far_s.shape).astype(BF16)
+    offer = cross(col_hot(flat(near_list[...]), nodes), node_ref[...])
+    near_s[...] = offer.reshape(near_s.shape).astype(BF16)
+    offer = cross(col_hot(flat(far_list[...]), nodes), node_ref[...])
+    far_s[...] = offer.reshape(far_s.shape).astype(BF16)
     out_swap.greet()
     out_swap.start()
 
@@ -697,9 +721,10 @@
     h_out[...] = (cross(hidden, delta) * node_scale).astype(BF16)
 
     halvings = []
-    for a in range(4):
-        slab, _ = outputs[a].shape
-        source = grads[a].reshape((2,) * bits + (slab, width))
+    for a in range(len(pieces)):
+        which, at = pieces[a]
+        slab = outputs[which].shape[0]
+        source = grads[which].reshape((2,) * bits + (slab, width))
         halvings.append(
             Halving(
                 turns[a],
@@ -708,13 +733,14 @@
                 source,
                 recv[a],
                 held[a],
-                outputs[a],
+                outputs[which],
                 send_sem.at[a],
                 recv_sem.at[a],
+                at if slab > 16 else None,
             )
         )
-    from_edges = (halvings[0], halvings[2])
-    from_nodes = (halvings[1], halvings[3])
+    from_edges = [item for item, (which, _) in zip(halvings, pieces) if which % 2 == 0]
+    from_nodes = [item for item, (which, _) in zip(halvings, pieces) if which % 2 == 1]
     for item in from_nodes:
         item.start()
     gg_s[...] = dot_t(pre_delta, v_b[...]).astype(BF16)
@@ -735,14 +761,13 @@
         acc_e[...] += cross(edge_s[span, :], pre_delta)
         return carry
 
-    half = steps // 2
-    lax.fori_loop(0, half, backward, 0)
-    for item in from_nodes:
-        item.step()
-    lax.fori_loop(half, steps, backward, 0)
-    for item in from_nodes:
-        item.step()
-
+    if steps <= 4:
+        for k in range(steps):
+            backward(k, 0)
+            for item in from_nodes:
+                item.step()
+    else:
+        lax.fori_loop(0, steps, backward, 0)
     g_in[pl.ds(0, width), :] = (acc_e[...] * edge_scale).astype(BF16)
     g_out[...] = (acc_o[...] * edge_scale).astype(BF16)
     own_sum = sums_s[pl.ds(0, nodes), :].astype(BF16)
@@ -779,7 +804,7 @@
     grad_edge_copy.wait()
 
 
-def whole(owner, node, ncot, code, recv_at, big, near_shape, far_shape, scales):
+def whole(near_list, far_list, node, ncot, code, recv_at, big, near_shape, far_shape, scales):
     row_bits = bit_count(lax.axis_size("row"))
     col_bits = bit_count(lax.axis_size("col"))
     bits = row_bits + col_bits
@@ -794,19 +819,20 @@
     along_col = list(range(bits - 2, row_bits - 1, -1))
     row_near = [row_bits - 1]
     row_far = list(range(row_bits - 2, -1, -1))
-    turns = [
+    pieces = [(a, at) for a in (1, 3, 0, 2) for at in range(0, slabs[a], 16)]
+    cycle = [
+        [core] + row_far + along_col + row_near,
+        [core] + row_near + row_far + along_col,
         [core] + along_col + row_near + row_far,
-        [core] + row_near + row_far + along_col,
-        [core] + row_near + row_far + along_col,
-        [core] + row_far + along_col + row_near,
     ]
+    turns = [cycle[k % 3] for k in range(len(pieces))]
     vmem = pl.BlockSpec(memory_space=pltpu.VMEM)
     anywhere = pl.BlockSpec(memory_space=pl.ANY)
     shape = jax.ShapeDtypeStruct
     dma = pltpu.SemaphoreType.DMA
     scratch = pltpu.VMEM
     return pl.pallas_call(
-        functools.partial(whole_kernel, tile, scales, turns, row_bits, col_bits),
+        functools.partial(whole_kernel, tile, scales, pieces, turns, row_bits, col_bits),
         name="whole_step",
         out_shape=(
             shape((nodes, width), BF16),
@@ -817,7 +843,7 @@
             shape(far_shape, BF16),
         )
         + tuple(shape((s, width), F32) for s in slabs),
-        in_specs=[vmem] * 5 + [anywhere] * 6,
+        in_specs=[vmem] * 6 + [anywhere] * 6,
         out_specs=[vmem, anywhere, anywhere] + [vmem] * 7,
         scratch_shapes=[
             scratch((rows + nodes, width), BF16),
@@ -836,16 +862,16 @@
         + [scratch(near_shape, BF16), scratch(far_shape, BF16)] * 3
         + [scratch(item, BF16) for item in grad_shapes]
         + [
-            scratch((2,) * (bits - 1 - phase) + (s, width), BF16)
-            for s in slabs
+            scratch((2,) * (bits - 1 - phase) + (16, width), BF16)
+            for _ in pieces
             for phase in range(bits)
         ]
         + [
-            scratch((2,) * (bits - 1 - phase) + (s, width), BF16)
-            for s in slabs
+            scratch((2,) * (bits - 1 - phase) + (16, width), BF16)
+            for _ in pieces
             for phase in range(bits - 1)
         ]
-        + [dma((4, bits)), dma((4, bits)), dma((6,)), dma((2,))]
+        + [dma((len(pieces), bits)), dma((len(pieces), bits)), dma((6,)), dma((2,))]
         + swap_sems(peers)
         + swap_sems(peers),
         compiler_params=pltpu.CompilerParams(
@@ -853,7 +879,8 @@
         ),
         cost_estimate=pl.CostEstimate(flops=10**10, bytes_accessed=10**8, transcendentals=0),
     )(
-        owner,
+        near_list,
+        far_list,
         node,
         ncot,
         code.reshape(edges // tile, 1, tile),
@@ -862,7 +889,7 @@
     )
 
 
-def close_kernel(count, owner_ref, part_ref, near_ref, far_ref, *refs):
+def close_kernel(count, near_list, far_list, part_ref, near_ref, far_ref, *refs):
     refs = list(refs)
     sums = refs[:4]
     passed = refs[4 : 4 + count]
@@ -881,10 +908,9 @@
     for copy in into:
         copy.start()
     nodes = part_ref.shape[0]
-    near = near_ref.shape[0]
-    hot = col_hot(owner_ref[...], nodes)
-    total = part_ref[...] + dot(hot[:, :near], near_ref[...])
-    grad_ref[...] = (total + dot(hot[:, near:], far_ref[...])).astype(BF16)
+    total = part_ref[...] + dot(col_hot(flat(near_list[...]), nodes), near_ref[...])
+    total += dot(col_hot(flat(far_list[...]), nodes), far_ref[...])
+    grad_ref[...] = total.astype(BF16)
     for source, target in zip(sums, targets):
         target[...] = source[...]
     for one, two in zip(into, out):
@@ -894,7 +920,7 @@
         copy.wait()
 
 
-def close(owner, part, near, far, sums, passed):
+def close(near_list, far_list, part, near, far, sums, passed):
     vmem = pl.BlockSpec(memory_space=pltpu.VMEM)
     anywhere = pl.BlockSpec(memory_space=pl.ANY)
     count = len(passed)
@@ -905,12 +931,12 @@
         out_shape=(shape(part.shape, BF16),)
         + tuple(shape(item.shape, F32) for item in sums)
         + tuple(shape(item.shape, BF16) for item in passed),
-        in_specs=[vmem] * 8 + [anywhere] * count,
+        in_specs=[vmem] * 9 + [anywhere] * count,
         out_specs=[vmem] * 5 + [anywhere] * count,
         scratch_shapes=[pltpu.VMEM(item.shape, BF16) for item in passed]
         + [pltpu.SemaphoreType.DMA((2, count))],
         compiler_params=pltpu.CompilerParams(vmem_limit_bytes=67043328),
-    )(owner, part, near, far, *sums, *passed)
+    )(near_list, far_list, part, near, far, *sums, *passed)
 
 
 def shards(
@@ -932,12 +958,12 @@
     peers = lax.axis_size("row") * lax.axis_size("col")
     near_shape = (4, near_list.shape[2], width)
     far_shape = (peers, far_list.shape[2], width)
-    owner = jnp.concatenate([near_list.reshape(-1), far_list.reshape(-1)], 0)[None, :]
     scales = (1.0 / math.sqrt(edge_rows * peers), 1.0 / math.sqrt(node_rows * peers))
     big = (edge_latent, edge_cotangent, w_edge_in, w_edge_out, w_node_in, w_node_out)
     if all(item.shape[0] % (16 * peers) == 0 for item in big[2:]):
         node_new, edge_new, grad_edge, part, near_back, far_back, *sums = whole(
-            owner,
+            near_list[0],
+            far_list[0],
             node_latent,
             node_cotangent,
             sender_code,
@@ -948,7 +974,8 @@
             scales,
         )
         grad_node, s_in, s_hin, s_out, s_hout, node_new, edge_new, grad_edge = close(
-            owner,
+            near_list[0],
+            far_list[0],
             part,
             near_back.reshape(-1, width),
             far_back.reshape(-1, width),
@@ -956,6 +983,7 @@
             (node_new, edge_new, grad_edge),
         )
         return (node_new, edge_new, grad_node, grad_edge, s_in, s_out, s_hin, s_hout)
+    owner = jnp.concatenate([near_list.reshape(-1), far_list.reshape(-1)], 0)[None, :]
     near, far = halo(owner, node_latent, near_shape, far_shape)
     node_new, edge_new, part, grad_edge, near_grad, far_grad, g_in, g_out, h_in, h_out = compute(
         node_latent,

time: 80.1 us -> 79.2 us (0.989); the launches traced: 79.9 us -> 78 us
  Pallas kernels: 77 us -> 75.8 us
    pallas_call x1, Pallas kernels: 71.2 us -> 69.9 us  [whole(): pl.pallas_call(functools.partial(whole_kernel, tile, scales, pieces, turn...]
    reshape x2 -> x0, local copies, waits for them, and re-layouts: 0.85 us -> none  [the longest x1 0.76 us: shards(): near_list.reshape(-1)]
where the time goes in v4:
time: 79.2 us; the launch traced here: 78 us
  Pallas kernels  75.8 us (96%)
  local copies, waits for them, and re-layouts  1.36 us (2%)
  between operations  0.8 us (1%)
    pallas_call x1, Pallas kernels, whole(): pl.pallas_call(functools.partial(whole_kernel, tile, scales, pieces, turn...  69.9 us
    pallas_call x1, Pallas kernels, close(): pl.pallas_call(functools.partial(close_kernel, count), name='close', out_...  5.9 us

profile of v4, /device:TPU:0, one launch (start us, length us, event | category | flops | bytes accessed | tf_op | source)
XLA Modules:
  0.0 78.0 jit_solution(433426473706450065)
XLA Ops:
  0.6 1.4 %copy.20 = s32[1,32,8]{2,1,0:T(8,128)} copy(s32[1,32,8]{1,2,0:T(8,128)} %param.23) | data formatting | bytes 2048 | tf_op args[11]
  2.0 69.9 %whole_step.1 = (bf16[256,512]{1,0:T(8,128)(2,1)}, bf16[2048,512]{1,0:T(8,128)(2,1)}, bf16[2048,512]{1,0:T(8,128)(2,1)}, f32[256,512]{1,0:T(8,128)}, bf16[4,64,5...) custom-call(s32[4,64]{1,0:T(4,128)} %bitcast.10, ...), custom_call_target="tpu_custom_call" | custom-call | flops 10000000000 | bytes 100000000 | tf_op jit(solution)/shard_map/whole_step/pallas_call | solution.py:834
  71.9 5.9 %close.1 = (bf16[256,512]{1,0:T(8,128)(2,1)}, f32[48,512]{1,0:T(8,128)}, f32[32,512]{1,0:T(8,128)}, f32[16,512]{1,0:T(8,128)}, f32[16,512]{1,0:T(8,128)}, /*inde...) custom-call(s32[4,64]{1,0:T(4,128)} %bitcast.11, s32[32,8]{1,0:T(8,128)} %bitcast.9, ...), custom_call_target="tpu_custom_call" | custom-call | tf_op jit(solution)/shard_map/close/pallas_call | solution.py:928
